TPU v7x, 32 devices: a whole 2x2x4 slice. The times are simulated.
32 devices in a mesh: scene: 2 (over y), pulse: 4 (over z), range: 2 (over x), rep: 2 (over core).
Axes of the slice: x: 2, y: 2, z: 4, core: 2. Of those that a mesh axis runs over, the one named last changes fastest.
Arguments:
- echo: bfloat16 [8, 64, 2, 6144], P(('scene', 'pulse'), 'rep', None, 'range'), parts along dimension 0, may hold values from -6 to 6
- chirp: bfloat16 [2, 512], replicated, may hold values from -0.1875 to 0.1875
- beam_one: int32 [2, 128], replicated, may hold values from 0 to 63, as said below
- shift_one: int32 [2, 128], replicated, may hold values from -28 to 28
- frac_one: float32 [2, 128], replicated, may hold values from 0 to 1
- base_one: float32 [2, 128], replicated, may hold values from -3.140625 to 3.140625
- beam_two: int32 [2, 256], replicated, may hold values from 0 to 127, as said below
- shift_two: int32 [2, 256], replicated, may hold values from -28 to 28
- frac_two: float32 [2, 256], replicated, may hold values from 0 to 1
- base_two: float32 [2, 256], replicated, may hold values from -3.140625 to 3.140625
Outputs:
- image: bfloat16 [2, 8, 32, 2, 6144], P('rep', ('scene', 'pulse'), None, None, 'range'), parts along dimension 1
There are 2 independent parts, one for each index of `scene`. A program takes and returns all parts, laid end to end along the dimension named above; an argument that names none is the same for every part. Nothing has to cross between parts.
Inputs may be any that keep to these rules, and one draw needn't show every extreme that they name: beam_one[c, p] differs from p // 2 by at most 1 and lies in the same aligned block of 8 child beams as p // 2; the first and last parent beams read child beams 0 and 63. beam_two[c, p] differs from p // 2 by at most 1 and lies in the same aligned block of 16 child beams as p // 2; the first and last parent beams read child beams 0 and 127.
All inputs are finite; a program needn't handle non-finite values.
Results may differ from a plain program's by a relative error of at most 0.012.
Values may be sent and summed in bfloat16 or wider, within the bound.
No kernel may reach another device: no remote copies, remote signals or barrier semaphores. Data moves between devices by JAX's collectives and lax.ppermute only.
A program may use at most 64 MiB of HBM per device.

v0:
```python
import jax
import jax.numpy as jnp
from jax import lax
from jax.experimental import pallas as pl
from jax.experimental.layout import Layout, with_layout_constraint
from jax.experimental.pallas import tpu as pltpu
from jax.sharding import PartitionSpec as P

LEFT = 128
STEP = 128
ROWS = 56
COLS = 64
GROUPS = 16
RIM = 32
WIDE = GROUPS * ROWS
SPANS = COLS // GROUPS
CHUNKS = ROWS // 8
BLOCKS = WIDE // STEP
ONE, TWO = 16, 32
TALL = ROWS + 2 * RIM
TOGETHER = 16


def position():
    rep, pulse = lax.axis_index("rep"), lax.axis_index("pulse")
    low, high = pulse % 2, pulse // 2 % 2
    return 4 * rep + 2 * low + high, low, high


def lane_ids(shape):
    return lax.broadcasted_iota(jnp.int32, shape, len(shape) - 1)


def row_ids(shape):
    return lax.broadcasted_iota(jnp.int32, shape, len(shape) - 2)


def exchange(parts):
    parts = list(parts)
    lane = lane_ids(parts[0].shape)
    step = 1
    while step < len(parts):
        low = (lane & step) == 0
        for first in range(len(parts)):
            if first & step:
                continue
            a, b = parts[first], parts[first + step]
            parts[first] = jnp.where(low, a, pltpu.roll(b, step, 1))
            parts[first + step] = jnp.where(low, pltpu.roll(a, 128 - step, 1), b)
        step *= 2
    return parts


def store_rimmed(ref, index, chunk, value):
    row = 8 * chunk
    ref[index, pl.ds(RIM + row, 8), :] = value
    if row >= ROWS - RIM:
        ref[index, pl.ds(row - (ROWS - RIM), 8), :] = pltpu.roll(value, 1, 1)
    if row < RIM:
        ref[index, pl.ds(RIM + ROWS + row, 8), :] = pltpu.roll(value, 127, 1)


def inside_test(bins):
    first_bin = lax.axis_index("range") * bins
    bin_total = bins * lax.axis_size("range")
    shape = (8, 128)
    place = (lane_ids(shape) & (COLS - 1)) * ROWS + row_ids(shape) + (first_bin - LEFT)

    def inside(chunk, value):
        spot = place + 8 * chunk
        return jnp.where((spot >= 0) & (spot < bin_total), value, 0.0)

    return inside


def fetch(sources, targets, sems):
    copies = [
        pltpu.make_async_copy(source, target, sems.at[index])
        for index, (source, target) in enumerate(zip(sources, targets))
    ]
    for copy in copies:
        copy.start()
    for copy in copies:
        copy.wait()


def prep_kernel(bins):
    def kernel(*refs):
        far, (band_ref, taps_ref, turn_ref) = refs[:7], refs[7:10]
        chirp_ref, shift_one, frac_one, base_one, shift_two, frac_two, base_two = refs[10:17]
        fetch(far, refs[10:17], refs[17])
        own, _, _ = position()
        first_bin = lax.axis_index("range") * bins
        bin_total = bins * lax.axis_size("range")
        span = band_ref.shape[0]
        for part in range(2):
            row = chirp_ref[part : part + 1, :].astype(jnp.float32)
            row = jnp.concatenate([row, jnp.zeros((1, STEP), jnp.float32)], axis=1)
            band = pltpu.roll(jnp.broadcast_to(row, (STEP, span)), 0, 1, stride=1, stride_axis=0)
            for block in range(span // 128):
                turned = band[:, 128 * block : 128 * block + 128].T
                band_ref[pl.ds(128 * block, 128), pl.ds(STEP * part, STEP)] = turned.astype(
                    jnp.bfloat16
                )

        shape = (8, 128)
        lane = lane_ids(shape)

        def packed(first, second):
            total = jnp.zeros(shape, jnp.float32)
            at = 0
            for ref, width in ((first, ONE), (second, TWO)):
                offset = own * width
                for child in range(2):
                    row = ref[child : child + 1, 0:128].astype(jnp.float32)
                    for block in range(1, ref.shape[1] // 128):
                        other = ref[child : child + 1, 128 * block : 128 * block + 128]
                        row = jnp.where(offset // 128 == block, other.astype(jnp.float32), row)
                    row = pltpu.roll(
                        jnp.broadcast_to(row, shape), (at + 256 - offset % 128) % 128, 1
                    )
                    total = jnp.where((lane >= at) & (lane < at + width), row, total)
                    at += width
            return total

        frac = packed(frac_one, frac_two)
        base = packed(base_one, base_two)
        slope = 0.5 * (packed(shift_one, shift_two) + frac)
        row = row_ids(shape).astype(jnp.float32)
        spread = (row - 3.0) - frac
        turned = jnp.pi * spread
        still = turned == 0.0
        safe = jnp.where(still, 1.0, turned)
        weights = jnp.where(still, 1.0, jnp.sin(safe) / safe) * (
            0.54 + 0.46 * jnp.cos(jnp.pi * spread / 4.0)
        )
        count = taps_ref.shape[0]
        square = (128, 128)
        base_rows = jnp.broadcast_to(base[0:1], square).T[:count]
        slope_rows = jnp.broadcast_to(slope[0:1], square).T[:count]
        wide = lane_ids((count, 128))
        spot = (wide & (COLS - 1)) * ROWS + (first_bin - LEFT)
        angle = base_rows + slope_rows * (spot.astype(jnp.float32) / bin_total - 0.5)
        cos_col, sin_col = jnp.cos(angle), jnp.sin(angle)
        sign = jnp.where(lane < COLS, -1.0, 1.0)
        fine, coarse = slope * (row / bin_total), slope * (8.0 / bin_total)
        cos_fine, sin_fine = jnp.cos(fine), jnp.sin(fine)
        cos_coarse, sin_coarse = jnp.cos(coarse), jnp.sin(coarse)
        for place in range(count):

            def spread_out(table):
                return jnp.broadcast_to(table[:, place : place + 1], shape)

            taps_ref[place] = spread_out(weights)
            cos_all = jnp.broadcast_to(cos_col[place : place + 1], shape)
            sin_all = jnp.broadcast_to(sin_col[place : place + 1], shape) * sign
            cos_step, sin_step = spread_out(cos_fine), spread_out(sin_fine) * sign
            cos_next, sin_next = spread_out(cos_coarse), spread_out(sin_coarse) * sign
            for chunk in range(CHUNKS):
                cos_all, sin_all = (
                    cos_all * cos_step - sin_all * sin_step,
                    sin_all * cos_step + cos_all * sin_step,
                )
                turn_ref[place, 0, pl.ds(8 * chunk, 8), :] = cos_all
                turn_ref[place, 1, pl.ds(8 * chunk, 8), :] = sin_all
                cos_step, sin_step = cos_next, sin_next

    return kernel


def compress_pair(near, far, bins, band_ref, source, columns, images, inside):
    rest = source.shape[2] - LEFT - bins
    wide = near[0].shape[2] - LEFT - bins

    def piece(held, comp, at, size):
        if len(held) == 1:
            return held[0][comp, :, pl.ds(at, size)]
        main, rim = held
        if at == LEFT:
            return main[comp]
        return rim[comp, :, pl.ds(min(at, LEFT), size)]

    for comp in range(2):
        for at, size in ((0, LEFT), (LEFT, bins), (LEFT + bins, wide)):
            sides = [piece(held, comp, at, size).astype(jnp.float32) for held in (near, far)]
            source[comp, :, pl.ds(at, size)] = jnp.concatenate(sides, axis=0).astype(jnp.bfloat16)
        if rest > wide:
            source[comp, :, pl.ds(LEFT + bins + wide, rest - wide)] = jnp.zeros(
                (16, rest - wide), jnp.bfloat16
            )
    span = band_ref.shape[0]
    windows = jnp.concatenate(
        [
            source[comp, :, pl.ds(WIDE * u + STEP * block, span)]
            for block in range(BLOCKS)
            for comp in range(2)
            for u in range(SPANS)
        ],
        axis=0,
    )
    product = jnp.dot(windows, band_ref[...], preferred_element_type=jnp.float32)
    half = 16 * SPANS
    for block in range(BLOCKS):
        top = product[128 * block : 128 * block + half]
        low = product[128 * block + half : 128 * block + 128]
        result = jnp.concatenate(
            [top[:, :STEP] + low[:, STEP:], low[:, :STEP] - top[:, STEP:]], axis=0
        )
        columns[pl.ds(STEP * block, STEP), :] = result.astype(jnp.bfloat16).T.astype(jnp.float32)
    for chunk in range(0, CHUNKS, 2):
        size = min(2, CHUNKS - chunk) * 8
        parts = [columns[pl.ds(ROWS * g + 8 * chunk, size), :] for g in range(GROUPS)]
        parts = exchange([part.astype(jnp.bfloat16) for part in parts])
        for image, part in enumerate(parts):
            part = part.astype(jnp.float32)
            for extra in range(size // 8):
                value = inside(chunk + extra, part[8 * extra : 8 * extra + 8])
                store_rimmed(images, image, chunk + extra, value)


def contribution(images, tables, parent, child, first_parent, first_image, width, at):
    beam_ref, shift_ref, taps_ref, turn_ref = tables
    place = at + child * width + parent
    image = beam_ref[child, first_parent + parent] + first_image
    start = shift_ref[child, first_parent + parent] + (RIM - 3)
    value = None
    for tap in range(8):
        term = images[image, pl.ds(start + tap, ROWS), :] * taps_ref[place, pl.ds(tap, 1), :]
        value = term if value is None else value + term
    parts = []
    for chunk in range(CHUNKS):
        part = value[8 * chunk : 8 * chunk + 8]
        parts.append(
            part * turn_ref[place, 0, pl.ds(8 * chunk, 8), :]
            + pltpu.roll(part, COLS, 1) * turn_ref[place, 1, pl.ds(8 * chunk, 8), :]
        )
    return parts


def loop_over(count, one):
    def step(index, carry):
        for extra in range(TOGETHER):
            one(TOGETHER * index + extra)
        return carry

    lax.fori_loop(0, count // TOGETHER, step, 0)


def merge_one(images, tables, result, inside):
    own, low, _ = position()

    def one(parent):
        sides = [
            contribution(
                images, tables, parent, child, ONE * own, (child ^ low) * 8 - 8 * own, ONE, 0
            )
            for child in range(2)
        ]
        for chunk, (a, b) in enumerate(zip(*sides)):
            store_rimmed(result, parent, chunk, inside(chunk, a + b))

    loop_over(ONE, one)


def second_side(images, tables, parent, child):
    own, _, _ = position()
    return contribution(images, tables, parent, child, TWO * own, -ONE * own, TWO, 2 * ONE)


def first_kernel(bins):
    def kernel(
        far_beam_one, far_shift_one, far_beam_two, far_shift_two, a0, a1, band_ref, taps_ref,
        turn_ref, out_ref, source, columns, images, level_one, beam_one, shift_one, beam_two,
        shift_two, sems,
    ):
        inside = inside_test(bins)
        fetch(
            (far_beam_one, far_shift_one, far_beam_two, far_shift_two),
            (beam_one, shift_one, beam_two, shift_two), sems,
        )
        compress_pair((a0,), (a1,), bins, band_ref, source, columns, images, inside)
        merge_one(images, (beam_one, shift_one, taps_ref, turn_ref), level_one, inside)
        _, _, high = position()
        tables = (beam_two, shift_two, taps_ref, turn_ref)

        def one(parent):
            for chunk, part in enumerate(second_side(level_one, tables, parent, high)):
                out_ref[parent, pl.ds(8 * chunk, 8), :] = part

        loop_over(TWO, one)

    return kernel


def second_kernel(bins):
    def kernel(
        far_beam_one, far_shift_one, far_beam_two, far_shift_two, a2, a3, r3, band_ref, taps_ref,
        turn_ref, half_ref, out_ref, source, columns, images, level_one, beam_one, shift_one,
        beam_two, shift_two, sems, level_two,
    ):
        inside = inside_test(bins)
        fetch(
            (far_beam_one, far_shift_one, far_beam_two, far_shift_two),
            (beam_one, shift_one, beam_two, shift_two), sems,
        )
        compress_pair((a2,), (a3, r3), bins, band_ref, source, columns, images, inside)
        merge_one(images, (beam_one, shift_one, taps_ref, turn_ref), level_one, inside)
        _, _, high = position()
        tables = (beam_two, shift_two, taps_ref, turn_ref)

        def one(parent):
            for chunk, part in enumerate(second_side(level_one, tables, parent, 1 - high)):
                rows = pl.ds(8 * chunk, 8)
                level_two[parent, rows, :] = part + half_ref[parent, rows, :]

        loop_over(TWO, one)
        for half in range(2):
            for chunk in range(0, CHUNKS, 2):
                size = min(2, CHUNKS - chunk) * 8
                parts = [
                    level_two[16 * half + image, pl.ds(8 * chunk, size), :].astype(jnp.bfloat16)
                    for image in range(GROUPS)
                ]
                for g, part in enumerate(exchange(parts)):
                    columns[pl.ds(ROWS * g + 8 * chunk, size), :] = part.astype(jnp.float32)
            for block in range(BLOCKS):
                turned = columns[pl.ds(STEP * block, STEP), :].astype(jnp.bfloat16).T
                for comp in range(2):
                    for u in range(SPANS):
                        left = WIDE * u + STEP * block - LEFT
                        if 0 <= left < bins:
                            row = (comp * SPANS + u) * 16
                            out_ref[comp, pl.ds(16 * half, 16), pl.ds(left, 128)] = turned[
                                row : row + 16
                            ]

    return kernel


def neighbours(head, tail, axis):
    count = lax.axis_size(axis)
    even = lax.axis_index(axis) % 2 == 0
    order = Layout(tuple(range(head.ndim)))
    near = [(i, i ^ 1) for i in range(count) if i ^ 1 < count]
    far = [(i + 1, i + 2) for i in range(0, count - 2, 2)]
    far = far + [(b, a) for a, b in far]
    first = with_layout_constraint(jnp.where(even, tail, head), order)
    first = with_layout_constraint(lax.ppermute(first, axis, near), order)
    second = lax.ppermute(jnp.where(even, head, tail), axis, far) if far else jnp.zeros_like(first)
    return jnp.where(even, second, first), jnp.where(even, first, second)


def body(
    echo, chirp, beam_one, shift_one, frac_one, base_one, beam_two, shift_two, frac_two, base_two
):
    signal = echo[0]
    beams, _, bins = signal.shape

    def split(array):
        return array.reshape(4, beams // 4, 2, array.shape[2]).transpose(0, 2, 1, 3)

    span = STEP + chirp.shape[1]
    pulse = lax.axis_index("pulse")

    from_left, from_right = (
        split(side) for side in neighbours(signal[:, :, :span], signal[:, :, bins - span :], "range")
    )
    signal = split(signal)
    small = (
        chirp, beam_one, shift_one, frac_one, base_one, beam_two, shift_two, frac_two, base_two
    )
    chirp, beam_one, shift_one, frac_one, base_one, beam_two, shift_two, frac_two, base_two = (
        pltpu.with_memory_space_constraint(array, pltpu.HBM) for array in small
    )

    def block_of(array, mask):
        index = pulse ^ mask
        return lax.dynamic_index_in_dim(array, 2 * (index % 2) + index // 2 % 2, 0, keepdims=False)

    def sent(array, mask):
        count = lax.axis_size("pulse")
        return lax.ppermute(array, "pulse", [(i, i ^ mask) for i in range(count)])

    far_main = sent(block_of(signal, 3), 3)
    from_left = from_left[:, :, :, span - LEFT :]
    wide = jnp.concatenate([from_left, signal, from_right], axis=3)
    rims = jnp.concatenate([from_left, from_right], axis=3)
    parts = [block_of(wide, 0)] + [sent(block_of(wide, mask), mask) for mask in (1, 2)]
    far_rim = sent(block_of(rims, 3), 3)

    vmem = pl.BlockSpec(memory_space=pltpu.VMEM)
    far = pl.BlockSpec(memory_space=pltpu.HBM)

    def held(space, *arrays):
        return [space(a.shape, a.dtype) for a in arrays] + [
            pltpu.SemaphoreType.DMA((len(arrays),))
        ]

    params = pltpu.CompilerParams(vmem_limit_bytes=24 << 20)
    count = 2 * (ONE + TWO)
    band, taps, turns = pl.pallas_call(
        prep_kernel(bins),
        out_shape=(
            jax.ShapeDtypeStruct((span, 2 * STEP), jnp.bfloat16),
            jax.ShapeDtypeStruct((count, 8, 128), jnp.float32),
            jax.ShapeDtypeStruct((count, 2, ROWS, 128), jnp.float32),
        ),
        in_specs=[far] * 7,
        out_specs=(vmem,) * 3,
        scratch_shapes=held(
            pltpu.VMEM, chirp, shift_one, frac_one, base_one, shift_two, frac_two, base_two
        ),
        compiler_params=params,
        name="prepare",
    )(chirp, shift_one, frac_one, base_one, shift_two, frac_two, base_two)

    index_tables = (beam_one, shift_one, beam_two, shift_two)
    scratch = [
        pltpu.VMEM((2, 16, SPANS * WIDE + span - STEP), jnp.bfloat16),
        pltpu.VMEM((WIDE, 128), jnp.float32),
        pltpu.VMEM((16, TALL, 128), jnp.float32),
        pltpu.VMEM((ONE, TALL, 128), jnp.float32),
    ] + held(pltpu.SMEM, *index_tables)
    half = pl.pallas_call(
        first_kernel(bins),
        out_shape=jax.ShapeDtypeStruct((TWO, ROWS, 128), jnp.float32),
        in_specs=[far] * 4 + [vmem] * 5,
        out_specs=vmem,
        scratch_shapes=scratch,
        compiler_params=params,
        name="first_pair",
    )(*index_tables, parts[0], parts[1], band, taps, turns)
    image = pl.pallas_call(
        second_kernel(bins),
        out_shape=jax.ShapeDtypeStruct((2, TWO, bins), jnp.bfloat16),
        in_specs=[far] * 4 + [vmem] * 7,
        out_specs=vmem,
        scratch_shapes=scratch + [pltpu.VMEM((TWO, ROWS, 128), jnp.float32)],
        compiler_params=params,
        name="second_pair",
    )(*index_tables, parts[2], far_main, far_rim, band, taps, turns, half)
    return image.transpose(1, 0, 2)[None, None]


def solution(mesh):
    in_specs = (P(("scene", "pulse"), "rep", None, "range"),) + (P(),) * 9
    out_specs = P("rep", ("scene", "pulse"), None, None, "range")

    return jax.shard_map(body, mesh=mesh, in_specs=in_specs, out_specs=out_specs, check_vma=False)
```

profile of v0, /device:TPU:0, one launch (start us, length us, event | category | flops | bytes accessed | tf_op | source)
XLA Modules:
  0.0 26.5 jit_solution(11252037247480500323)
XLA Ops:
  0.0 1.0 %broadcast_select_fusion.2 = bf16[32,2,640]{2,1,0:T(2,128)(2,1)S(1)} fusion(pred[]{:T(512)S(6)} %eq.15, bf16[32,2,3072]{2,1,0:T(2,128)(2,1)} %bitcast.35), kind=kLoop, calls=%fused_computation.5 | loop fusion | flops 40960 | bytes 245761 | tf_op jit(solution)/shard_map/jit(_where)/select_n | solution.py:347
  1.0 3.0 %collective-permute-start = (bf16[32,2,640]{2,1,0:T(2,128)(2,1)S(1)}, bf16[32,2,640]{2,1,0:T(2,128)(2,1)S(1)}, u32[]{:S(2)}, u32[]{:S(2)}) collective-permute-start(bf16[32,2,640]{2,1,0:T(2,128)(2,1)S(1)} %broadcast_select_fusion.2), channel_id=1, source_target_pairs={{0,2},{2,0},{1,3},{3,1},{4,6},{6,4},{5,7},{7,5},{8,10},{10,8},{9,1... | collective-permute-start | bytes 245768 | tf_op jit(solution)/shard_map/ppermute | solution.py:348
  4.1 1.1 %copy.22 = bf16[1,32,2,3072]{3,1,2,0:T(8,128)(2,1)S(1)} copy(bf16[1,32,2,3072]{3,2,1,0:T(2,128)(2,1)} %param.10) | data formatting | bytes 786432 | tf_op args[0]
  5.2 3.7 %collective-permute-start.2 = (bf16[2,8,3072]{2,1,0:T(8,128)(2,1)S(1)}, bf16[2,8,3072]{2,1,0:T(8,128)(2,1)S(1)}, u32[]{:S(2)}, u32[]{:S(2)}) collective-permute-start(bf16[2,8,3072]{2,1,0:T(8,128)(2,1)S(1)} %dynamic-slice_bitcast_fusion.3), channel_id=1, source_target_pairs={{0,12},{4,8},{8,4},{12,0},{1,13},{5,9},{9,5},{13,1},{2,14},{6,10},... | collective-permute-start | bytes 294920 | tf_op jit(solution)/shard_map/ppermute | solution.py:382
  8.8 0.0 collective-permute-done
  8.8 0.1 broadcast_select_fusion.1
  9.1 0.1 collective-permute-start.4
  9.2 2.3 %collective-permute-start.1 = (bf16[2,8,3840]{2,1,0:T(8,128)(2,1)S(1)}, bf16[2,8,3840]{2,1,0:T(8,128)(2,1)S(1)}, u32[]{:S(2)}, u32[]{:S(2)}) collective-permute-start(bf16[2,8,3840]{2,1,0:T(8,128)(2,1)S(1)} %get-tuple-element.13), channel_id=1, source_target_pairs={{0,8},{4,12},{8,0},{12,4},{1,9},{5,13},{9,1},{13,5},{2,10},{6,14},... | collective-permute-start | bytes 368648 | tf_op jit(solution)/shard_map/ppermute | solution.py:382
  11.5 2.1 %collective-permute-start.3 = (bf16[2,8,768]{2,1,0:T(8,128)(2,1)S(1)}, bf16[2,8,768]{2,1,0:T(8,128)(2,1)S(1)}, u32[]{:S(2)}, u32[]{:S(2)}) collective-permute-start(bf16[2,8,768]{2,1,0:T(8,128)(2,1)S(1)} %fusion.1), channel_id=1, source_target_pairs={{0,12},{4,8},{8,4},{12,0},{1,13},{5,9},{9,5},{13,1},{2,14},{6,10},... | collective-permute-start | bytes 73736 | tf_op jit(solution)/shard_map/ppermute | solution.py:382
  13.6 2.1 %prepare.1 = (bf16[640,256]{1,0:T(8,128)(2,1)S(1)}, f32[96,8,128]{2,1,0:T(8,128)S(1)}, f32[96,2,56,128]{3,2,1,0:T(8,128)S(1)}) custom-call(bf16[2,512]{1,0:T(2,128)(2,1)} %refs_0_.1, s32[2,128]{1,0:T(2,128)} %far_shift_one.3, f32[2,128]{1,0:T(2,128)} %refs_2_.1, f32[2,128]{1,0:T(2,128)} %refs_3_.1, s32[2,256]{1,0:T(2,128)} %far_shift_two.3, ...), custom_call_target="tpu_custom_call" | custom-call | tf_op jit(solution)/shard_map/prepare/pallas_call | solution.py:401
  15.7 0.8 %collective-permute-done.4.a1 = bf16[2,8,3840]{2,1,0:T(8,128)(2,1)S(1)} collective-permute-done((bf16[2,8,3840]{2,1,0:T(8,128)(2,1)S(1)}, bf16[2,8,3840]{2,1,0:T(8,128)(2,1)S(1)}, u32[]{:S(2)}, u32[]{:S(2)}) %collective-permute-start.4) | collective-permute-done | bytes 122912 | tf_op jit(solution)/shard_map/ppermute | solution.py:382
  16.5 3.5 %first_pair.1.half_ref = f32[32,56,128]{2,1,0:T(8,128)S(1)} custom-call(s32[2,128]{1,0:T(2,128)} %far_beam_one.3, s32[2,128]{1,0:T(2,128)} %far_shift_one.3, s32[2,256]{1,0:T(2,128)} %far_beam_two.3, s32[2,256]{1,0:T(2,128)} %far_shift_two.3, bf16[2,8,3840]{2,1,0:T(8,128)(2,1)S(1)} %get-tuple-element.12.a0, ...), custom_call_target="tpu_custom_call" | custom-call | tf_op jit(solution)/shard_map/first_pair/pallas_call | solution.py:424
  20.0 0.0 collective-permute-done.2.a3
  20.1 0.0 collective-permute-done.3.r3
  20.1 0.0 collective-permute-done.1.a2
  20.1 5.3 %second_pair.1 = bf16[2,32,3072]{2,1,0:T(8,128)(2,1)S(1)} custom-call(s32[2,128]{1,0:T(2,128)} %far_beam_one.3, s32[2,128]{1,0:T(2,128)} %far_shift_one.3, s32[2,256]{1,0:T(2,128)} %far_beam_two.3, s32[2,256]{1,0:T(2,128)} %far_shift_two.3, bf16[2,8,3840]{2,1,0:T(8,128)(2,1)S(1)} %collective-permute-done.1.a2, ...), custom_call_target="tpu_custom_call" | custom-call | tf_op jit(solution)/shard_map/second_pair/pallas_call | solution.py:433
  25.4 1.2 %copy.16 = bf16[1,1,32,2,3072]{4,3,2,1,0:T(2,128)(2,1)} copy(bf16[1,1,32,2,3072]{4,2,3,1,0:T(8,128)(2,1)S(1)} %bitcast.32) | data formatting | bytes 786432 | tf_op jit(solution)/shard_map/broadcast_in_dim | solution.py:442
  (6 shorter events, 0.1 us)
Async XLA Ops:
  1.0 7.8 %collective-permute-start = (bf16[32,2,640]{2,1,0:T(2,128)(2,1)S(1)}, bf16[32,2,640]{2,1,0:T(2,128)(2,1)S(1)}, u32[]{:S(2)}, u32[]{:S(2)}) collective-permute-start(bf16[32,2,640]{2,1,0:T(2,128)(2,1)S(1)} %broadcast_select_fusion.2), channel_id=1, source_target_pairs={{0,2},{2,0},{1,3},{3,1},{4,6},{6,4},{5,7},{7,5},{8,10},{10,8},{9,1... | collective-permute-start | bytes 245768 | tf_op jit(solution)/shard_map/ppermute | solution.py:348
  5.2 14.9 %collective-permute-start.2 = (bf16[2,8,3072]{2,1,0:T(8,128)(2,1)S(1)}, bf16[2,8,3072]{2,1,0:T(8,128)(2,1)S(1)}, u32[]{:S(2)}, u32[]{:S(2)}) collective-permute-start(bf16[2,8,3072]{2,1,0:T(8,128)(2,1)S(1)} %dynamic-slice_bitcast_fusion.3), channel_id=1, source_target_pairs={{0,12},{4,8},{8,4},{12,0},{1,13},{5,9},{9,5},{13,1},{2,14},{6,10},... | collective-permute-start | bytes 294920 | tf_op jit(solution)/shard_map/ppermute | solution.py:382
  9.1 7.4 %collective-permute-start.4 = (bf16[2,8,3840]{2,1,0:T(8,128)(2,1)S(1)}, bf16[2,8,3840]{2,1,0:T(8,128)(2,1)S(1)}, u32[]{:S(2)}, u32[]{:S(2)}) collective-permute-start(bf16[2,8,3840]{2,1,0:T(8,128)(2,1)S(1)} %get-tuple-element.11), channel_id=1, source_target_pairs={{0,4},{4,0},{8,12},{12,8},{1,5},{5,1},{9,13},{13,9},{2,6},{6,2},{1... | collective-permute-start | bytes 368648 | tf_op jit(solution)/shard_map/ppermute | solution.py:382
  9.2 10.9 %collective-permute-start.1 = (bf16[2,8,3840]{2,1,0:T(8,128)(2,1)S(1)}, bf16[2,8,3840]{2,1,0:T(8,128)(2,1)S(1)}, u32[]{:S(2)}, u32[]{:S(2)}) collective-permute-start(bf16[2,8,3840]{2,1,0:T(8,128)(2,1)S(1)} %get-tuple-element.13), channel_id=1, source_target_pairs={{0,8},{4,12},{8,0},{12,4},{1,9},{5,13},{9,1},{13,5},{2,10},{6,14},... | collective-permute-start | bytes 368648 | tf_op jit(solution)/shard_map/ppermute | solution.py:382
  11.5 8.6 %collective-permute-start.3 = (bf16[2,8,768]{2,1,0:T(8,128)(2,1)S(1)}, bf16[2,8,768]{2,1,0:T(8,128)(2,1)S(1)}, u32[]{:S(2)}, u32[]{:S(2)}) collective-permute-start(bf16[2,8,768]{2,1,0:T(8,128)(2,1)S(1)} %fusion.1), channel_id=1, source_target_pairs={{0,12},{4,8},{8,4},{12,0},{1,13},{5,9},{9,5},{13,1},{2,14},{6,10},... | collective-permute-start | bytes 73736 | tf_op jit(solution)/shard_map/ppermute | solution.py:382
where the time goes:
time: 26.8 us; the launch traced here: 26.5 us
  starting transfers between devices  11.1 us (41%)
  Pallas kernels  10.9 us (41%)
  local copies, waits for them, and re-layouts  2.29 us (9%)
  other arithmetic  1.18 us (4%)
  waiting for transfers between devices  0.85 us (3%)
    ppermute x4, starting transfers between devices, sent(): return lax.ppermute(array, 'pulse', [(i, i ^ mask) for i in range(count)])  8.11 us
    pallas_call x1, Pallas kernels, body(): pl.pallas_call(second_kernel(bins), out_shape=jax.ShapeDtypeStruct((2, TW...  5.28 us
    pallas_call x1, Pallas kernels, body(): pl.pallas_call(first_kernel(bins), out_shape=jax.ShapeDtypeStruct((TWO, R...  3.52 us
    ppermute x1, starting transfers between devices, neighbours(): first = with_layout_constraint(lax.ppermute(first, axis, near), order)  3.03 us
    pallas_call x1, Pallas kernels, body(): pl.pallas_call(prep_kernel(bins), out_shape=(jax.ShapeDtypeStruct((span,...  2.11 us
    broadcast_in_dim x1, local copies, waits for them, and re-layouts, body(): return image.transpose(1, 0, 2)[None, None]  1.15 us
    unnamed x1, local copies, waits for them, and re-layouts  1.06 us
    select_n x1, other arithmetic, neighbours(): first = with_layout_constraint(jnp.where(even, tail, head), order)  1.02 us
  transfers between devices with their start and end apart: 5, of which 1 were waited for; matrix products, arithmetic and copies ran while one was open for 5% of the time, Pallas kernels for 21%

commit v1 on v0

--- a/solution.py
+++ b/solution.py
@@ -2,7 +2,6 @@
 import jax.numpy as jnp
 from jax import lax
 from jax.experimental import pallas as pl
-from jax.experimental.layout import Layout, with_layout_constraint
 from jax.experimental.pallas import tpu as pltpu
 from jax.sharding import PartitionSpec as P
 
@@ -340,12 +339,10 @@
 def neighbours(head, tail, axis):
     count = lax.axis_size(axis)
     even = lax.axis_index(axis) % 2 == 0
-    order = Layout(tuple(range(head.ndim)))
     near = [(i, i ^ 1) for i in range(count) if i ^ 1 < count]
     far = [(i + 1, i + 2) for i in range(0, count - 2, 2)]
     far = far + [(b, a) for a, b in far]
-    first = with_layout_constraint(jnp.where(even, tail, head), order)
-    first = with_layout_constraint(lax.ppermute(first, axis, near), order)
+    first = lax.ppermute(jnp.where(even, tail, head), axis, near)
     second = lax.ppermute(jnp.where(even, head, tail), axis, far) if far else jnp.zeros_like(first)
     return jnp.where(even, second, first), jnp.where(even, first, second)
 
@@ -355,17 +352,10 @@
 ):
     signal = echo[0]
     beams, _, bins = signal.shape
-
-    def split(array):
-        return array.reshape(4, beams // 4, 2, array.shape[2]).transpose(0, 2, 1, 3)
-
     span = STEP + chirp.shape[1]
     pulse = lax.axis_index("pulse")
 
-    from_left, from_right = (
-        split(side) for side in neighbours(signal[:, :, :span], signal[:, :, bins - span :], "range")
-    )
-    signal = split(signal)
+    signal = signal.reshape(4, beams // 4, 2, bins).transpose(0, 2, 1, 3)
     small = (
         chirp, beam_one, shift_one, frac_one, base_one, beam_two, shift_two, frac_two, base_two
     )
@@ -382,6 +372,9 @@
         return lax.ppermute(array, "pulse", [(i, i ^ mask) for i in range(count)])
 
     far_main = sent(block_of(signal, 3), 3)
+    from_left, from_right = neighbours(
+        signal[:, :, :, :span], signal[:, :, :, bins - span :], "range"
+    )
     from_left = from_left[:, :, :, span - LEFT :]
     wide = jnp.concatenate([from_left, signal, from_right], axis=3)
     rims = jnp.concatenate([from_left, from_right], axis=3)

time: 26.8 us -> 25.4 us (0.948)
  other arithmetic: 1.18 us -> 0.08 us
    select_n x1, other arithmetic: 1.02 us -> 0.02 us  [neighbours(): first = lax.ppermute(jnp.where(even, tail, head), axis, near)]
  transfers between devices with their start and end apart: 5 -> 5, of which waited for: 1 -> 1; matrix products, arithmetic and copies ran while one was open for 5% -> 0% of each run, Pallas kernels for 21% -> 22%
where the time goes in v1:
time: 25.4 us; the launch traced here: 25.2 us
  starting transfers between devices  11.1 us (44%)
  Pallas kernels  10.9 us (43%)
  local copies, waits for them, and re-layouts  2.26 us (9%)
  waiting for transfers between devices  0.66 us (3%)
    ppermute x4, starting transfers between devices, sent(): return lax.ppermute(array, 'pulse', [(i, i ^ mask) for i in range(count)])  8.11 us
    pallas_call x1, Pallas kernels, body(): pl.pallas_call(second_kernel(bins), out_shape=jax.ShapeDtypeStruct((2, TW...  5.28 us
    pallas_call x1, Pallas kernels, body(): pl.pallas_call(first_kernel(bins), out_shape=jax.ShapeDtypeStruct((TWO, R...  3.52 us
    ppermute x1, starting transfers between devices, neighbours(): first = lax.ppermute(jnp.where(even, tail, head), axis, near)  3.03 us
    pallas_call x1, Pallas kernels, body(): pl.pallas_call(prep_kernel(bins), out_shape=(jax.ShapeDtypeStruct((span,...  2.11 us
    broadcast_in_dim x1, local copies, waits for them, and re-layouts, body(): return image.transpose(1, 0, 2)[None, None]  1.15 us
    unnamed x1, local copies, waits for them, and re-layouts  1.06 us
    ppermute x4, waiting for transfers between devices, sent(): return lax.ppermute(array, 'pulse', [(i, i ^ mask) for i in range(count)])  0.66 us
  transfers between devices with their start and end apart: 5, of which 1 were waited for; matrix products, arithmetic and copies ran while one was open for 0% of the time, Pallas kernels for 22%

profile of v1, /device:TPU:0, one launch (start us, length us, event | category | flops | bytes accessed | tf_op | source)
XLA Modules:
  0.0 25.2 jit_solution(15801893330753328550)
XLA Ops:
  0.0 1.1 %copy.18 = bf16[1,32,2,3072]{3,1,2,0:T(8,128)(2,1)S(1)} copy(bf16[1,32,2,3072]{3,2,1,0:T(2,128)(2,1)} %param.10) | data formatting | bytes 786432 | tf_op args[0]
  1.1 3.0 %collective-permute-start = (bf16[4,2,8,640]{3,2,0,1:T(8,128)(2,1)S(1)}, bf16[4,2,8,640]{3,2,0,1:T(8,128)(2,1)S(1)}, u32[]{:S(2)}, u32[]{:S(2)}) collective-permute-start(bf16[4,2,8,640]{3,2,0,1:T(8,128)(2,1)S(1)} %slice_select_fusion), channel_id=1, source_target_pairs={{0,2},{2,0},{1,3},{3,1},{4,6},{6,4},{5,7},{7,5},{8,10},{10,8},{9,1... | collective-permute-start | bytes 245768 | tf_op jit(solution)/shard_map/ppermute | solution.py:345
  4.1 3.7 %collective-permute-start.2 = (bf16[2,8,3072]{2,1,0:T(8,128)(2,1)S(1)}, bf16[2,8,3072]{2,1,0:T(8,128)(2,1)S(1)}, u32[]{:S(2)}, u32[]{:S(2)}) collective-permute-start(bf16[2,8,3072]{2,1,0:T(8,128)(2,1)S(1)} %dynamic-slice_bitcast_fusion.3), channel_id=1, source_target_pairs={{0,12},{4,8},{8,4},{12,0},{1,13},{5,9},{9,5},{13,1},{2,14},{6,10},... | collective-permute-start | bytes 294920 | tf_op jit(solution)/shard_map/ppermute | solution.py:372
  7.8 0.0 collective-permute-done
  7.9 0.9 %collective-permute-start.4 = (bf16[2,8,3840]{2,1,0:T(8,128)(2,1)S(1)}, bf16[2,8,3840]{2,1,0:T(8,128)(2,1)S(1)}, u32[]{:S(2)}, u32[]{:S(2)}) collective-permute-start(bf16[2,8,3840]{2,1,0:T(8,128)(2,1)S(1)} %get-tuple-element.11), channel_id=1, source_target_pairs={{0,4},{4,0},{8,12},{12,8},{1,5},{5,1},{9,13},{13,9},{2,6},{6,2},{1... | collective-permute-start | bytes 368648 | tf_op jit(solution)/shard_map/ppermute | solution.py:372
  8.8 2.6 %collective-permute-start.1 = (bf16[2,8,3840]{2,1,0:T(8,128)(2,1)S(1)}, bf16[2,8,3840]{2,1,0:T(8,128)(2,1)S(1)}, u32[]{:S(2)}, u32[]{:S(2)}) collective-permute-start(bf16[2,8,3840]{2,1,0:T(8,128)(2,1)S(1)} %get-tuple-element.13), channel_id=1, source_target_pairs={{0,8},{4,12},{8,0},{12,4},{1,9},{5,13},{9,1},{13,5},{2,10},{6,14},... | collective-permute-start | bytes 368648 | tf_op jit(solution)/shard_map/ppermute | solution.py:372
  11.4 0.9 %collective-permute-start.3 = (bf16[2,8,768]{2,1,0:T(8,128)(2,1)S(1)}, bf16[2,8,768]{2,1,0:T(8,128)(2,1)S(1)}, u32[]{:S(2)}, u32[]{:S(2)}) collective-permute-start(bf16[2,8,768]{2,1,0:T(8,128)(2,1)S(1)} %fusion.1), channel_id=1, source_target_pairs={{0,12},{4,8},{8,4},{12,0},{1,13},{5,9},{9,5},{13,1},{2,14},{6,10},... | collective-permute-start | bytes 73736 | tf_op jit(solution)/shard_map/ppermute | solution.py:372
  12.4 2.1 %prepare.1 = (bf16[640,256]{1,0:T(8,128)(2,1)S(1)}, f32[96,8,128]{2,1,0:T(8,128)S(1)}, f32[96,2,56,128]{3,2,1,0:T(8,128)S(1)}) custom-call(bf16[2,512]{1,0:T(2,128)(2,1)} %refs_0_.1, s32[2,128]{1,0:T(2,128)} %far_shift_one.3, f32[2,128]{1,0:T(2,128)} %refs_2_.1, f32[2,128]{1,0:T(2,128)} %refs_3_.1, s32[2,256]{1,0:T(2,128)} %far_shift_two.3, ...), custom_call_target="tpu_custom_call" | custom-call | tf_op jit(solution)/shard_map/prepare/pallas_call | solution.py:394
  14.5 0.7 %collective-permute-done.4.a1 = bf16[2,8,3840]{2,1,0:T(8,128)(2,1)S(1)} collective-permute-done((bf16[2,8,3840]{2,1,0:T(8,128)(2,1)S(1)}, bf16[2,8,3840]{2,1,0:T(8,128)(2,1)S(1)}, u32[]{:S(2)}, u32[]{:S(2)}) %collective-permute-start.4) | collective-permute-done | bytes 122912 | tf_op jit(solution)/shard_map/ppermute | solution.py:372
  15.1 3.5 %first_pair.1.half_ref = f32[32,56,128]{2,1,0:T(8,128)S(1)} custom-call(s32[2,128]{1,0:T(2,128)} %far_beam_one.3, s32[2,128]{1,0:T(2,128)} %far_shift_one.3, s32[2,256]{1,0:T(2,128)} %far_beam_two.3, s32[2,256]{1,0:T(2,128)} %far_shift_two.3, bf16[2,8,3840]{2,1,0:T(8,128)(2,1)S(1)} %get-tuple-element.12.a0, ...), custom_call_target="tpu_custom_call" | custom-call | tf_op jit(solution)/shard_map/first_pair/pallas_call | solution.py:417
  18.7 0.0 collective-permute-done.2.a3
  18.7 0.0 collective-permute-done.3.r3
  18.7 0.0 collective-permute-done.1.a2
  18.7 5.3 %second_pair.1 = bf16[2,32,3072]{2,1,0:T(8,128)(2,1)S(1)} custom-call(s32[2,128]{1,0:T(2,128)} %far_beam_one.3, s32[2,128]{1,0:T(2,128)} %far_shift_one.3, s32[2,256]{1,0:T(2,128)} %far_beam_two.3, s32[2,256]{1,0:T(2,128)} %far_shift_two.3, bf16[2,8,3840]{2,1,0:T(8,128)(2,1)S(1)} %collective-permute-done.1.a2, ...), custom_call_target="tpu_custom_call" | custom-call | tf_op jit(solution)/shard_map/second_pair/pallas_call | solution.py:426
  24.0 1.2 %copy.14 = bf16[1,1,32,2,3072]{4,3,2,1,0:T(2,128)(2,1)} copy(bf16[1,1,32,2,3072]{4,2,3,1,0:T(8,128)(2,1)S(1)} %bitcast.23) | data formatting | bytes 786432 | tf_op jit(solution)/shard_map/broadcast_in_dim | solution.py:435
  (7 shorter events, 0.1 us)
Async XLA Ops:
  1.1 6.7 %collective-permute-start = (bf16[4,2,8,640]{3,2,0,1:T(8,128)(2,1)S(1)}, bf16[4,2,8,640]{3,2,0,1:T(8,128)(2,1)S(1)}, u32[]{:S(2)}, u32[]{:S(2)}) collective-permute-start(bf16[4,2,8,640]{3,2,0,1:T(8,128)(2,1)S(1)} %slice_select_fusion), channel_id=1, source_target_pairs={{0,2},{2,0},{1,3},{3,1},{4,6},{6,4},{5,7},{7,5},{8,10},{10,8},{9,1... | collective-permute-start | bytes 245768 | tf_op jit(solution)/shard_map/ppermute | solution.py:345
  4.1 14.5 %collective-permute-start.2 = (bf16[2,8,3072]{2,1,0:T(8,128)(2,1)S(1)}, bf16[2,8,3072]{2,1,0:T(8,128)(2,1)S(1)}, u32[]{:S(2)}, u32[]{:S(2)}) collective-permute-start(bf16[2,8,3072]{2,1,0:T(8,128)(2,1)S(1)} %dynamic-slice_bitcast_fusion.3), channel_id=1, source_target_pairs={{0,12},{4,8},{8,4},{12,0},{1,13},{5,9},{9,5},{13,1},{2,14},{6,10},... | collective-permute-start | bytes 294920 | tf_op jit(solution)/shard_map/ppermute | solution.py:372
  7.9 7.2 %collective-permute-start.4 = (bf16[2,8,3840]{2,1,0:T(8,128)(2,1)S(1)}, bf16[2,8,3840]{2,1,0:T(8,128)(2,1)S(1)}, u32[]{:S(2)}, u32[]{:S(2)}) collective-permute-start(bf16[2,8,3840]{2,1,0:T(8,128)(2,1)S(1)} %get-tuple-element.11), channel_id=1, source_target_pairs={{0,4},{4,0},{8,12},{12,8},{1,5},{5,1},{9,13},{13,9},{2,6},{6,2},{1... | collective-permute-start | bytes 368648 | tf_op jit(solution)/shard_map/ppermute | solution.py:372
  8.8 9.9 %collective-permute-start.1 = (bf16[2,8,3840]{2,1,0:T(8,128)(2,1)S(1)}, bf16[2,8,3840]{2,1,0:T(8,128)(2,1)S(1)}, u32[]{:S(2)}, u32[]{:S(2)}) collective-permute-start(bf16[2,8,3840]{2,1,0:T(8,128)(2,1)S(1)} %get-tuple-element.13), channel_id=1, source_target_pairs={{0,8},{4,12},{8,0},{12,4},{1,9},{5,13},{9,1},{13,5},{2,10},{6,14},... | collective-permute-start | bytes 368648 | tf_op jit(solution)/shard_map/ppermute | solution.py:372
  11.4 7.3 %collective-permute-start.3 = (bf16[2,8,768]{2,1,0:T(8,128)(2,1)S(1)}, bf16[2,8,768]{2,1,0:T(8,128)(2,1)S(1)}, u32[]{:S(2)}, u32[]{:S(2)}) collective-permute-start(bf16[2,8,768]{2,1,0:T(8,128)(2,1)S(1)} %fusion.1), channel_id=1, source_target_pairs={{0,12},{4,8},{8,4},{12,0},{1,13},{5,9},{9,5},{13,1},{2,14},{6,10},... | collective-permute-start | bytes 73736 | tf_op jit(solution)/shard_map/ppermute | solution.py:372

commit v2 on v1

--- a/solution.py
+++ b/solution.py
@@ -268,7 +268,7 @@
 
 def first_kernel(bins):
     def kernel(
-        far_beam_one, far_shift_one, far_beam_two, far_shift_two, a0, a1, band_ref, taps_ref,
+        far_beam_one, far_shift_one, far_beam_two, far_shift_two, a0, a1, r1, band_ref, taps_ref,
         turn_ref, out_ref, source, columns, images, level_one, beam_one, shift_one, beam_two,
         shift_two, sems,
     ):
@@ -277,7 +277,7 @@
             (far_beam_one, far_shift_one, far_beam_two, far_shift_two),
             (beam_one, shift_one, beam_two, shift_two), sems,
         )
-        compress_pair((a0,), (a1,), bins, band_ref, source, columns, images, inside)
+        compress_pair((a0,), (a1, r1), bins, band_ref, source, columns, images, inside)
         merge_one(images, (beam_one, shift_one, taps_ref, turn_ref), level_one, inside)
         _, _, high = position()
         tables = (beam_two, shift_two, taps_ref, turn_ref)
@@ -372,13 +372,15 @@
         return lax.ppermute(array, "pulse", [(i, i ^ mask) for i in range(count)])
 
     far_main = sent(block_of(signal, 3), 3)
+    near_main = sent(block_of(signal, 1), 1)
     from_left, from_right = neighbours(
         signal[:, :, :, :span], signal[:, :, :, bins - span :], "range"
     )
     from_left = from_left[:, :, :, span - LEFT :]
     wide = jnp.concatenate([from_left, signal, from_right], axis=3)
     rims = jnp.concatenate([from_left, from_right], axis=3)
-    parts = [block_of(wide, 0)] + [sent(block_of(wide, mask), mask) for mask in (1, 2)]
+    near_rim = sent(block_of(rims, 1), 1)
+    middle = sent(block_of(wide, 2), 2)
     far_rim = sent(block_of(rims, 3), 3)
 
     vmem = pl.BlockSpec(memory_space=pltpu.VMEM)
@@ -417,12 +419,12 @@
     half = pl.pallas_call(
         first_kernel(bins),
         out_shape=jax.ShapeDtypeStruct((TWO, ROWS, 128), jnp.float32),
-        in_specs=[far] * 4 + [vmem] * 5,
+        in_specs=[far] * 4 + [vmem] * 6,
         out_specs=vmem,
         scratch_shapes=scratch,
         compiler_params=params,
         name="first_pair",
-    )(*index_tables, parts[0], parts[1], band, taps, turns)
+    )(*index_tables, block_of(wide, 0), near_main, near_rim, band, taps, turns)
     image = pl.pallas_call(
         second_kernel(bins),
         out_shape=jax.ShapeDtypeStruct((2, TWO, bins), jnp.bfloat16),
@@ -431,7 +433,7 @@
         scratch_shapes=scratch + [pltpu.VMEM((TWO, ROWS, 128), jnp.float32)],
         compiler_params=params,
         name="second_pair",
-    )(*index_tables, parts[2], far_main, far_rim, band, taps, turns, half)
+    )(*index_tables, middle, far_main, far_rim, band, taps, turns, half)
     return image.transpose(1, 0, 2)[None, None]
 
 

time: 25.4 us -> 25.4 us (level)
  starting transfers between devices: 11.1 us -> 11.6 us
  waiting for transfers between devices: 0.66 us -> 0.25 us
    ppermute x4 -> x5, starting transfers between devices: 8.11 us -> 8.57 us  [sent(): return lax.ppermute(array, 'pulse', [(i, i ^ mask) for i in range(count)])]
    ppermute x4 -> x5, waiting for transfers between devices: 0.66 us -> 0.25 us  [sent(): return lax.ppermute(array, 'pulse', [(i, i ^ mask) for i in range(count)])]
  transfers between devices with their start and end apart: 5 -> 6, of which waited for: 1 -> 1; matrix products, arithmetic and copies ran while one was open for 0% -> 0% of each run, Pallas kernels for 22% -> 22%
where the time goes in v2:
time: 25.4 us; the launch traced here: 25.2 us
  starting transfers between devices  11.6 us (46%)
  Pallas kernels  10.9 us (43%)
  local copies, waits for them, and re-layouts  2.26 us (9%)
    ppermute x5, starting transfers between devices, sent(): return lax.ppermute(array, 'pulse', [(i, i ^ mask) for i in range(count)])  8.57 us
    pallas_call x1, Pallas kernels, body(): pl.pallas_call(second_kernel(bins), out_shape=jax.ShapeDtypeStruct((2, TW...  5.28 us
    pallas_call x1, Pallas kernels, body(): pl.pallas_call(first_kernel(bins), out_shape=jax.ShapeDtypeStruct((TWO, R...  3.53 us
    ppermute x1, starting transfers between devices, neighbours(): first = lax.ppermute(jnp.where(even, tail, head), axis, near)  3.03 us
    pallas_call x1, Pallas kernels, body(): pl.pallas_call(prep_kernel(bins), out_shape=(jax.ShapeDtypeStruct((span,...  2.11 us
    broadcast_in_dim x1, local copies, waits for them, and re-layouts, body(): return image.transpose(1, 0, 2)[None, None]  1.15 us
    unnamed x1, local copies, waits for them, and re-layouts  1.06 us
  transfers between devices with their start and end apart: 6, of which 1 were waited for; matrix products, arithmetic and copies ran while one was open for 0% of the time, Pallas kernels for 22%

profile of v2, /device:TPU:0, one launch (start us, length us, event | category | flops | bytes accessed | tf_op | source)
XLA Modules:
  0.0 25.2 jit_solution(10231044360861075578)
XLA Ops:
  0.0 1.1 %copy.20 = bf16[1,32,2,3072]{3,1,2,0:T(8,128)(2,1)S(1)} copy(bf16[1,32,2,3072]{3,2,1,0:T(2,128)(2,1)} %param.10) | data formatting | bytes 786432 | tf_op args[0]
  1.1 3.0 %collective-permute-start = (bf16[4,2,8,640]{3,2,0,1:T(8,128)(2,1)S(1)}, bf16[4,2,8,640]{3,2,0,1:T(8,128)(2,1)S(1)}, u32[]{:S(2)}, u32[]{:S(2)}) collective-permute-start(bf16[4,2,8,640]{3,2,0,1:T(8,128)(2,1)S(1)} %slice_select_fusion), channel_id=1, source_target_pairs={{0,2},{2,0},{1,3},{3,1},{4,6},{6,4},{5,7},{7,5},{8,10},{10,8},{9,1... | collective-permute-start | bytes 245768 | tf_op jit(solution)/shard_map/ppermute | solution.py:345
  4.1 1.6 %collective-permute-start.4 = (bf16[2,8,3072]{2,1,0:T(8,128)(2,1)S(1)}, bf16[2,8,3072]{2,1,0:T(8,128)(2,1)S(1)}, u32[]{:S(2)}, u32[]{:S(2)}) collective-permute-start(bf16[2,8,3072]{2,1,0:T(8,128)(2,1)S(1)} %get-tuple-element.13), channel_id=1, source_target_pairs={{0,4},{4,0},{8,12},{12,8},{1,5},{5,1},{9,13},{13,9},{2,6},{6,2},{1... | collective-permute-start | bytes 294920 | tf_op jit(solution)/shard_map/ppermute | solution.py:372
  5.8 2.5 %collective-permute-start.2 = (bf16[2,8,3072]{2,1,0:T(8,128)(2,1)S(1)}, bf16[2,8,3072]{2,1,0:T(8,128)(2,1)S(1)}, u32[]{:S(2)}, u32[]{:S(2)}) collective-permute-start(bf16[2,8,3072]{2,1,0:T(8,128)(2,1)S(1)} %get-tuple-element.14), channel_id=1, source_target_pairs={{0,12},{4,8},{8,4},{12,0},{1,13},{5,9},{9,5},{13,1},{2,14},{6,10},... | collective-permute-start | bytes 294920 | tf_op jit(solution)/shard_map/ppermute | solution.py:372
  8.3 0.0 collective-permute-done
  8.4 1.5 %collective-permute-start.1 = (bf16[2,8,3840]{2,1,0:T(8,128)(2,1)S(1)}, bf16[2,8,3840]{2,1,0:T(8,128)(2,1)S(1)}, u32[]{:S(2)}, u32[]{:S(2)}) collective-permute-start(bf16[2,8,3840]{2,1,0:T(8,128)(2,1)S(1)} %get-tuple-element.12), channel_id=1, source_target_pairs={{0,8},{4,12},{8,0},{12,4},{1,9},{5,13},{9,1},{13,5},{2,10},{6,14},... | collective-permute-start | bytes 368648 | tf_op jit(solution)/shard_map/ppermute | solution.py:372
  9.8 1.6 %collective-permute-start.5 = (bf16[2,8,768]{2,1,0:T(8,128)(2,1)S(1)}, bf16[2,8,768]{2,1,0:T(8,128)(2,1)S(1)}, u32[]{:S(2)}, u32[]{:S(2)}) collective-permute-start(bf16[2,8,768]{2,1,0:T(8,128)(2,1)S(1)} %get-tuple-element.17), channel_id=1, source_target_pairs={{0,4},{4,0},{8,12},{12,8},{1,5},{5,1},{9,13},{13,9},{2,6},{6,2},{1... | collective-permute-start | bytes 73736 | tf_op jit(solution)/shard_map/ppermute | solution.py:372
  11.4 1.4 %collective-permute-start.3 = (bf16[2,8,768]{2,1,0:T(8,128)(2,1)S(1)}, bf16[2,8,768]{2,1,0:T(8,128)(2,1)S(1)}, u32[]{:S(2)}, u32[]{:S(2)}) collective-permute-start(bf16[2,8,768]{2,1,0:T(8,128)(2,1)S(1)} %get-tuple-element.18), channel_id=1, source_target_pairs={{0,12},{4,8},{8,4},{12,0},{1,13},{5,9},{9,5},{13,1},{2,14},{6,10},... | collective-permute-start | bytes 73736 | tf_op jit(solution)/shard_map/ppermute | solution.py:372
  12.8 2.1 %prepare.1 = (bf16[640,256]{1,0:T(8,128)(2,1)S(1)}, f32[96,8,128]{2,1,0:T(8,128)S(1)}, f32[96,2,56,128]{3,2,1,0:T(8,128)S(1)}) custom-call(bf16[2,512]{1,0:T(2,128)(2,1)} %refs_0_.1, s32[2,128]{1,0:T(2,128)} %far_shift_one.3, f32[2,128]{1,0:T(2,128)} %refs_2_.1, f32[2,128]{1,0:T(2,128)} %refs_3_.1, s32[2,256]{1,0:T(2,128)} %far_shift_two.3, ...), custom_call_target="tpu_custom_call" | custom-call | tf_op jit(solution)/shard_map/prepare/pallas_call | solution.py:396
  14.9 0.0 collective-permute-done.4.a1
  15.0 0.0 collective-permute-done.5.r1
  15.0 3.5 %first_pair.1.half_ref = f32[32,56,128]{2,1,0:T(8,128)S(1)} custom-call(s32[2,128]{1,0:T(2,128)} %far_beam_one.3, s32[2,128]{1,0:T(2,128)} %far_shift_one.3, s32[2,256]{1,0:T(2,128)} %far_beam_two.3, s32[2,256]{1,0:T(2,128)} %far_shift_two.3, bf16[2,8,3840]{2,1,0:T(8,128)(2,1)S(1)} %get-tuple-element.11.a0, ...), custom_call_target="tpu_custom_call" | custom-call | tf_op jit(solution)/shard_map/first_pair/pallas_call | solution.py:419
  18.5 0.0 collective-permute-done.2.a3
  18.5 0.0 collective-permute-done.3.r3
  18.5 0.2 collective-permute-done.1.a2
  18.8 5.3 %second_pair.1 = bf16[2,32,3072]{2,1,0:T(8,128)(2,1)S(1)} custom-call(s32[2,128]{1,0:T(2,128)} %far_beam_one.3, s32[2,128]{1,0:T(2,128)} %far_shift_one.3, s32[2,256]{1,0:T(2,128)} %far_beam_two.3, s32[2,256]{1,0:T(2,128)} %far_shift_two.3, bf16[2,8,3840]{2,1,0:T(8,128)(2,1)S(1)} %collective-permute-done.1.a2, ...), custom_call_target="tpu_custom_call" | custom-call | tf_op jit(solution)/shard_map/second_pair/pallas_call | solution.py:428
  24.1 1.2 %copy.15 = bf16[1,1,32,2,3072]{4,3,2,1,0:T(2,128)(2,1)} copy(bf16[1,1,32,2,3072]{4,2,3,1,0:T(8,128)(2,1)S(1)} %bitcast.29) | data formatting | bytes 786432 | tf_op jit(solution)/shard_map/broadcast_in_dim | solution.py:437
  (7 shorter events, 0.1 us)
Async XLA Ops:
  1.1 7.2 %collective-permute-start = (bf16[4,2,8,640]{3,2,0,1:T(8,128)(2,1)S(1)}, bf16[4,2,8,640]{3,2,0,1:T(8,128)(2,1)S(1)}, u32[]{:S(2)}, u32[]{:S(2)}) collective-permute-start(bf16[4,2,8,640]{3,2,0,1:T(8,128)(2,1)S(1)} %slice_select_fusion), channel_id=1, source_target_pairs={{0,2},{2,0},{1,3},{3,1},{4,6},{6,4},{5,7},{7,5},{8,10},{10,8},{9,1... | collective-permute-start | bytes 245768 | tf_op jit(solution)/shard_map/ppermute | solution.py:345
  4.1 10.8 %collective-permute-start.4 = (bf16[2,8,3072]{2,1,0:T(8,128)(2,1)S(1)}, bf16[2,8,3072]{2,1,0:T(8,128)(2,1)S(1)}, u32[]{:S(2)}, u32[]{:S(2)}) collective-permute-start(bf16[2,8,3072]{2,1,0:T(8,128)(2,1)S(1)} %get-tuple-element.13), channel_id=1, source_target_pairs={{0,4},{4,0},{8,12},{12,8},{1,5},{5,1},{9,13},{13,9},{2,6},{6,2},{1... | collective-permute-start | bytes 294920 | tf_op jit(solution)/shard_map/ppermute | solution.py:372
  5.8 12.7 %collective-permute-start.2 = (bf16[2,8,3072]{2,1,0:T(8,128)(2,1)S(1)}, bf16[2,8,3072]{2,1,0:T(8,128)(2,1)S(1)}, u32[]{:S(2)}, u32[]{:S(2)}) collective-permute-start(bf16[2,8,3072]{2,1,0:T(8,128)(2,1)S(1)} %get-tuple-element.14), channel_id=1, source_target_pairs={{0,12},{4,8},{8,4},{12,0},{1,13},{5,9},{9,5},{13,1},{2,14},{6,10},... | collective-permute-start | bytes 294920 | tf_op jit(solution)/shard_map/ppermute | solution.py:372
  8.4 10.4 %collective-permute-start.1 = (bf16[2,8,3840]{2,1,0:T(8,128)(2,1)S(1)}, bf16[2,8,3840]{2,1,0:T(8,128)(2,1)S(1)}, u32[]{:S(2)}, u32[]{:S(2)}) collective-permute-start(bf16[2,8,3840]{2,1,0:T(8,128)(2,1)S(1)} %get-tuple-element.12), channel_id=1, source_target_pairs={{0,8},{4,12},{8,0},{12,4},{1,9},{5,13},{9,1},{13,5},{2,10},{6,14},... | collective-permute-start | bytes 368648 | tf_op jit(solution)/shard_map/ppermute | solution.py:372
  9.8 5.1 %collective-permute-start.5 = (bf16[2,8,768]{2,1,0:T(8,128)(2,1)S(1)}, bf16[2,8,768]{2,1,0:T(8,128)(2,1)S(1)}, u32[]{:S(2)}, u32[]{:S(2)}) collective-permute-start(bf16[2,8,768]{2,1,0:T(8,128)(2,1)S(1)} %get-tuple-element.17), channel_id=1, source_target_pairs={{0,4},{4,0},{8,12},{12,8},{1,5},{5,1},{9,13},{13,9},{2,6},{6,2},{1... | collective-permute-start | bytes 73736 | tf_op jit(solution)/shard_map/ppermute | solution.py:372
  11.4 7.1 %collective-permute-start.3 = (bf16[2,8,768]{2,1,0:T(8,128)(2,1)S(1)}, bf16[2,8,768]{2,1,0:T(8,128)(2,1)S(1)}, u32[]{:S(2)}, u32[]{:S(2)}) collective-permute-start(bf16[2,8,768]{2,1,0:T(8,128)(2,1)S(1)} %get-tuple-element.18), channel_id=1, source_target_pairs={{0,12},{4,8},{8,4},{12,0},{1,13},{5,9},{9,5},{13,1},{2,14},{6,10},... | collective-permute-start | bytes 73736 | tf_op jit(solution)/shard_map/ppermute | solution.py:372

commit v3 on v1

--- a/solution.py
+++ b/solution.py
@@ -79,6 +79,10 @@
     ]
     for copy in copies:
         copy.start()
+    return copies
+
+
+def arrived(copies):
     for copy in copies:
         copy.wait()
 
@@ -87,11 +91,12 @@
     def kernel(*refs):
         far, (band_ref, taps_ref, turn_ref) = refs[:7], refs[7:10]
         chirp_ref, shift_one, frac_one, base_one, shift_two, frac_two, base_two = refs[10:17]
-        fetch(far, refs[10:17], refs[17])
+        copies = fetch(far, refs[10:17], refs[17])
         own, _, _ = position()
         first_bin = lax.axis_index("range") * bins
         bin_total = bins * lax.axis_size("range")
         span = band_ref.shape[0]
+        arrived(copies[:1])
         for part in range(2):
             row = chirp_ref[part : part + 1, :].astype(jnp.float32)
             row = jnp.concatenate([row, jnp.zeros((1, STEP), jnp.float32)], axis=1)
@@ -102,6 +107,7 @@
                     jnp.bfloat16
                 )
 
+        arrived(copies[1:])
         shape = (8, 128)
         lane = lane_ids(shape)
 
@@ -273,11 +279,12 @@
         shift_two, sems,
     ):
         inside = inside_test(bins)
-        fetch(
+        copies = fetch(
             (far_beam_one, far_shift_one, far_beam_two, far_shift_two),
             (beam_one, shift_one, beam_two, shift_two), sems,
         )
         compress_pair((a0,), (a1,), bins, band_ref, source, columns, images, inside)
+        arrived(copies)
         merge_one(images, (beam_one, shift_one, taps_ref, turn_ref), level_one, inside)
         _, _, high = position()
         tables = (beam_two, shift_two, taps_ref, turn_ref)
@@ -298,11 +305,12 @@
         beam_two, shift_two, sems, level_two,
     ):
         inside = inside_test(bins)
-        fetch(
+        copies = fetch(
             (far_beam_one, far_shift_one, far_beam_two, far_shift_two),
             (beam_one, shift_one, beam_two, shift_two), sems,
         )
         compress_pair((a2,), (a3, r3), bins, band_ref, source, columns, images, inside)
+        arrived(copies)
         merge_one(images, (beam_one, shift_one, taps_ref, turn_ref), level_one, inside)
         _, _, high = position()
         tables = (beam_two, shift_two, taps_ref, turn_ref)

time: 25.4 us -> 24.9 us (0.980)
  Pallas kernels: 10.9 us -> 10.5 us
    pallas_call x1, Pallas kernels: 5.28 us -> 4.85 us  [body(): pl.pallas_call(second_kernel(bins), out_shape=jax.ShapeDtypeStruct((2, TW...]
  transfers between devices with their start and end apart: 5 -> 5, of which waited for: 1 -> 1; matrix products, arithmetic and copies ran while one was open for 0% -> 0% of each run, Pallas kernels for 22% -> 23%
where the time goes in v3:
time: 24.9 us; the launch traced here: 24.7 us
  starting transfers between devices  11.1 us (45%)
  Pallas kernels  10.5 us (42%)
  local copies, waits for them, and re-layouts  2.26 us (9%)
  waiting for transfers between devices  0.68 us (3%)
    ppermute x4, starting transfers between devices, sent(): return lax.ppermute(array, 'pulse', [(i, i ^ mask) for i in range(count)])  8.11 us
    pallas_call x1, Pallas kernels, body(): pl.pallas_call(second_kernel(bins), out_shape=jax.ShapeDtypeStruct((2, TW...  4.85 us
    pallas_call x1, Pallas kernels, body(): pl.pallas_call(first_kernel(bins), out_shape=jax.ShapeDtypeStruct((TWO, R...  3.53 us
    ppermute x1, starting transfers between devices, neighbours(): first = lax.ppermute(jnp.where(even, tail, head), axis, near)  3.03 us
    pallas_call x1, Pallas kernels, body(): pl.pallas_call(prep_kernel(bins), out_shape=(jax.ShapeDtypeStruct((span,...  2.09 us
    broadcast_in_dim x1, local copies, waits for them, and re-layouts, body(): return image.transpose(1, 0, 2)[None, None]  1.15 us
    unnamed x1, local copies, waits for them, and re-layouts  1.06 us
    ppermute x4, waiting for transfers between devices, sent(): return lax.ppermute(array, 'pulse', [(i, i ^ mask) for i in range(count)])  0.68 us
  transfers between devices with their start and end apart: 5, of which 1 were waited for; matrix products, arithmetic and copies ran while one was open for 0% of the time, Pallas kernels for 23%

profile of v3, /device:TPU:0, one launch (start us, length us, event | category | flops | bytes accessed | tf_op | source)
XLA Modules:
  0.0 24.7 jit_solution(10982544553909053749)
XLA Ops:
  0.0 1.1 %copy.18 = bf16[1,32,2,3072]{3,1,2,0:T(8,128)(2,1)S(1)} copy(bf16[1,32,2,3072]{3,2,1,0:T(2,128)(2,1)} %param.10) | data formatting | bytes 786432 | tf_op args[0]
  1.1 3.0 %collective-permute-start = (bf16[4,2,8,640]{3,2,0,1:T(8,128)(2,1)S(1)}, bf16[4,2,8,640]{3,2,0,1:T(8,128)(2,1)S(1)}, u32[]{:S(2)}, u32[]{:S(2)}) collective-permute-start(bf16[4,2,8,640]{3,2,0,1:T(8,128)(2,1)S(1)} %slice_select_fusion), channel_id=1, source_target_pairs={{0,2},{2,0},{1,3},{3,1},{4,6},{6,4},{5,7},{7,5},{8,10},{10,8},{9,1... | collective-permute-start | bytes 245768 | tf_op jit(solution)/shard_map/ppermute | solution.py:353
  4.1 3.7 %collective-permute-start.2 = (bf16[2,8,3072]{2,1,0:T(8,128)(2,1)S(1)}, bf16[2,8,3072]{2,1,0:T(8,128)(2,1)S(1)}, u32[]{:S(2)}, u32[]{:S(2)}) collective-permute-start(bf16[2,8,3072]{2,1,0:T(8,128)(2,1)S(1)} %dynamic-slice_bitcast_fusion.3), channel_id=1, source_target_pairs={{0,12},{4,8},{8,4},{12,0},{1,13},{5,9},{9,5},{13,1},{2,14},{6,10},... | collective-permute-start | bytes 294920 | tf_op jit(solution)/shard_map/ppermute | solution.py:380
  7.8 0.0 collective-permute-done
  7.9 0.9 %collective-permute-start.4 = (bf16[2,8,3840]{2,1,0:T(8,128)(2,1)S(1)}, bf16[2,8,3840]{2,1,0:T(8,128)(2,1)S(1)}, u32[]{:S(2)}, u32[]{:S(2)}) collective-permute-start(bf16[2,8,3840]{2,1,0:T(8,128)(2,1)S(1)} %get-tuple-element.11), channel_id=1, source_target_pairs={{0,4},{4,0},{8,12},{12,8},{1,5},{5,1},{9,13},{13,9},{2,6},{6,2},{1... | collective-permute-start | bytes 368648 | tf_op jit(solution)/shard_map/ppermute | solution.py:380
  8.8 2.6 %collective-permute-start.1 = (bf16[2,8,3840]{2,1,0:T(8,128)(2,1)S(1)}, bf16[2,8,3840]{2,1,0:T(8,128)(2,1)S(1)}, u32[]{:S(2)}, u32[]{:S(2)}) collective-permute-start(bf16[2,8,3840]{2,1,0:T(8,128)(2,1)S(1)} %get-tuple-element.13), channel_id=1, source_target_pairs={{0,8},{4,12},{8,0},{12,4},{1,9},{5,13},{9,1},{13,5},{2,10},{6,14},... | collective-permute-start | bytes 368648 | tf_op jit(solution)/shard_map/ppermute | solution.py:380
  11.4 0.9 %collective-permute-start.3 = (bf16[2,8,768]{2,1,0:T(8,128)(2,1)S(1)}, bf16[2,8,768]{2,1,0:T(8,128)(2,1)S(1)}, u32[]{:S(2)}, u32[]{:S(2)}) collective-permute-start(bf16[2,8,768]{2,1,0:T(8,128)(2,1)S(1)} %fusion.1), channel_id=1, source_target_pairs={{0,12},{4,8},{8,4},{12,0},{1,13},{5,9},{9,5},{13,1},{2,14},{6,10},... | collective-permute-start | bytes 73736 | tf_op jit(solution)/shard_map/ppermute | solution.py:380
  12.4 2.1 %prepare.1 = (bf16[640,256]{1,0:T(8,128)(2,1)S(1)}, f32[96,8,128]{2,1,0:T(8,128)S(1)}, f32[96,2,56,128]{3,2,1,0:T(8,128)S(1)}) custom-call(bf16[2,512]{1,0:T(2,128)(2,1)} %refs_0_.1, s32[2,128]{1,0:T(2,128)} %far_shift_one.3, f32[2,128]{1,0:T(2,128)} %refs_2_.1, f32[2,128]{1,0:T(2,128)} %refs_3_.1, s32[2,256]{1,0:T(2,128)} %far_shift_two.3, ...), custom_call_target="tpu_custom_call" | custom-call | tf_op jit(solution)/shard_map/prepare/pallas_call | solution.py:402
  14.5 0.7 %collective-permute-done.4.a1 = bf16[2,8,3840]{2,1,0:T(8,128)(2,1)S(1)} collective-permute-done((bf16[2,8,3840]{2,1,0:T(8,128)(2,1)S(1)}, bf16[2,8,3840]{2,1,0:T(8,128)(2,1)S(1)}, u32[]{:S(2)}, u32[]{:S(2)}) %collective-permute-start.4) | collective-permute-done | bytes 122912 | tf_op jit(solution)/shard_map/ppermute | solution.py:380
  15.1 3.5 %first_pair.1.half_ref = f32[32,56,128]{2,1,0:T(8,128)S(1)} custom-call(s32[2,128]{1,0:T(2,128)} %far_beam_one.3, s32[2,128]{1,0:T(2,128)} %far_shift_one.3, s32[2,256]{1,0:T(2,128)} %far_beam_two.3, s32[2,256]{1,0:T(2,128)} %far_shift_two.3, bf16[2,8,3840]{2,1,0:T(8,128)(2,1)S(1)} %get-tuple-element.12.a0, ...), custom_call_target="tpu_custom_call" | custom-call | tf_op jit(solution)/shard_map/first_pair/pallas_call | solution.py:425
  18.7 0.0 collective-permute-done.2.a3
  18.7 0.0 collective-permute-done.3.r3
  18.7 0.0 collective-permute-done.1.a2
  18.7 4.9 %second_pair.1 = bf16[2,32,3072]{2,1,0:T(8,128)(2,1)S(1)} custom-call(s32[2,128]{1,0:T(2,128)} %far_beam_one.3, s32[2,128]{1,0:T(2,128)} %far_shift_one.3, s32[2,256]{1,0:T(2,128)} %far_beam_two.3, s32[2,256]{1,0:T(2,128)} %far_shift_two.3, bf16[2,8,3840]{2,1,0:T(8,128)(2,1)S(1)} %collective-permute-done.1.a2, ...), custom_call_target="tpu_custom_call" | custom-call | tf_op jit(solution)/shard_map/second_pair/pallas_call | solution.py:434
  23.6 1.2 %copy.14 = bf16[1,1,32,2,3072]{4,3,2,1,0:T(2,128)(2,1)} copy(bf16[1,1,32,2,3072]{4,2,3,1,0:T(8,128)(2,1)S(1)} %bitcast.23) | data formatting | bytes 786432 | tf_op jit(solution)/shard_map/broadcast_in_dim | solution.py:443
  (7 shorter events, 0.1 us)
Async XLA Ops:
  1.1 6.7 %collective-permute-start = (bf16[4,2,8,640]{3,2,0,1:T(8,128)(2,1)S(1)}, bf16[4,2,8,640]{3,2,0,1:T(8,128)(2,1)S(1)}, u32[]{:S(2)}, u32[]{:S(2)}) collective-permute-start(bf16[4,2,8,640]{3,2,0,1:T(8,128)(2,1)S(1)} %slice_select_fusion), channel_id=1, source_target_pairs={{0,2},{2,0},{1,3},{3,1},{4,6},{6,4},{5,7},{7,5},{8,10},{10,8},{9,1... | collective-permute-start | bytes 245768 | tf_op jit(solution)/shard_map/ppermute | solution.py:353
  4.1 14.6 %collective-permute-start.2 = (bf16[2,8,3072]{2,1,0:T(8,128)(2,1)S(1)}, bf16[2,8,3072]{2,1,0:T(8,128)(2,1)S(1)}, u32[]{:S(2)}, u32[]{:S(2)}) collective-permute-start(bf16[2,8,3072]{2,1,0:T(8,128)(2,1)S(1)} %dynamic-slice_bitcast_fusion.3), channel_id=1, source_target_pairs={{0,12},{4,8},{8,4},{12,0},{1,13},{5,9},{9,5},{13,1},{2,14},{6,10},... | collective-permute-start | bytes 294920 | tf_op jit(solution)/shard_map/ppermute | solution.py:380
  7.9 7.2 %collective-permute-start.4 = (bf16[2,8,3840]{2,1,0:T(8,128)(2,1)S(1)}, bf16[2,8,3840]{2,1,0:T(8,128)(2,1)S(1)}, u32[]{:S(2)}, u32[]{:S(2)}) collective-permute-start(bf16[2,8,3840]{2,1,0:T(8,128)(2,1)S(1)} %get-tuple-element.11), channel_id=1, source_target_pairs={{0,4},{4,0},{8,12},{12,8},{1,5},{5,1},{9,13},{13,9},{2,6},{6,2},{1... | collective-permute-start | bytes 368648 | tf_op jit(solution)/shard_map/ppermute | solution.py:380
  8.8 9.9 %collective-permute-start.1 = (bf16[2,8,3840]{2,1,0:T(8,128)(2,1)S(1)}, bf16[2,8,3840]{2,1,0:T(8,128)(2,1)S(1)}, u32[]{:S(2)}, u32[]{:S(2)}) collective-permute-start(bf16[2,8,3840]{2,1,0:T(8,128)(2,1)S(1)} %get-tuple-element.13), channel_id=1, source_target_pairs={{0,8},{4,12},{8,0},{12,4},{1,9},{5,13},{9,1},{13,5},{2,10},{6,14},... | collective-permute-start | bytes 368648 | tf_op jit(solution)/shard_map/ppermute | solution.py:380
  11.4 7.3 %collective-permute-start.3 = (bf16[2,8,768]{2,1,0:T(8,128)(2,1)S(1)}, bf16[2,8,768]{2,1,0:T(8,128)(2,1)S(1)}, u32[]{:S(2)}, u32[]{:S(2)}) collective-permute-start(bf16[2,8,768]{2,1,0:T(8,128)(2,1)S(1)} %fusion.1), channel_id=1, source_target_pairs={{0,12},{4,8},{8,4},{12,0},{1,13},{5,9},{9,5},{13,1},{2,14},{6,10},... | collective-permute-start | bytes 73736 | tf_op jit(solution)/shard_map/ppermute | solution.py:380

commit v4 on v3

--- a/solution.py
+++ b/solution.py
@@ -274,7 +274,7 @@
 
 def first_kernel(bins):
     def kernel(
-        far_beam_one, far_shift_one, far_beam_two, far_shift_two, a0, a1, band_ref, taps_ref,
+        far_beam_one, far_shift_one, far_beam_two, far_shift_two, a0, a1, r1, band_ref, taps_ref,
         turn_ref, out_ref, source, columns, images, level_one, beam_one, shift_one, beam_two,
         shift_two, sems,
     ):
@@ -283,7 +283,7 @@
             (far_beam_one, far_shift_one, far_beam_two, far_shift_two),
             (beam_one, shift_one, beam_two, shift_two), sems,
         )
-        compress_pair((a0,), (a1,), bins, band_ref, source, columns, images, inside)
+        compress_pair((a0,), (a1, r1), bins, band_ref, source, columns, images, inside)
         arrived(copies)
         merge_one(images, (beam_one, shift_one, taps_ref, turn_ref), level_one, inside)
         _, _, high = position()
@@ -380,13 +380,15 @@
         return lax.ppermute(array, "pulse", [(i, i ^ mask) for i in range(count)])
 
     far_main = sent(block_of(signal, 3), 3)
+    near_main = sent(block_of(signal, 1), 1)
     from_left, from_right = neighbours(
         signal[:, :, :, :span], signal[:, :, :, bins - span :], "range"
     )
     from_left = from_left[:, :, :, span - LEFT :]
     wide = jnp.concatenate([from_left, signal, from_right], axis=3)
     rims = jnp.concatenate([from_left, from_right], axis=3)
-    parts = [block_of(wide, 0)] + [sent(block_of(wide, mask), mask) for mask in (1, 2)]
+    middle = sent(block_of(wide, 2), 2)
+    near_rim = sent(block_of(rims, 1), 1)
     far_rim = sent(block_of(rims, 3), 3)
 
     vmem = pl.BlockSpec(memory_space=pltpu.VMEM)
@@ -425,12 +427,12 @@
     half = pl.pallas_call(
         first_kernel(bins),
         out_shape=jax.ShapeDtypeStruct((TWO, ROWS, 128), jnp.float32),
-        in_specs=[far] * 4 + [vmem] * 5,
+        in_specs=[far] * 4 + [vmem] * 6,
         out_specs=vmem,
         scratch_shapes=scratch,
         compiler_params=params,
         name="first_pair",
-    )(*index_tables, parts[0], parts[1], band, taps, turns)
+    )(*index_tables, block_of(wide, 0), near_main, near_rim, band, taps, turns)
     image = pl.pallas_call(
         second_kernel(bins),
         out_shape=jax.ShapeDtypeStruct((2, TWO, bins), jnp.bfloat16),
@@ -439,7 +441,7 @@
         scratch_shapes=scratch + [pltpu.VMEM((TWO, ROWS, 128), jnp.float32)],
         compiler_params=params,
         name="second_pair",
-    )(*index_tables, parts[2], far_main, far_rim, band, taps, turns, half)
+    )(*index_tables, middle, far_main, far_rim, band, taps, turns, half)
     return image.transpose(1, 0, 2)[None, None]
 
 

time: 24.9 us -> 25 us (level)
  starting transfers between devices: 11.1 us -> 11.6 us
  waiting for transfers between devices: 0.68 us -> 0.26 us
    ppermute x4 -> x5, starting transfers between devices: 8.11 us -> 8.57 us  [sent(): return lax.ppermute(array, 'pulse', [(i, i ^ mask) for i in range(count)])]
    ppermute x4 -> x5, waiting for transfers between devices: 0.68 us -> 0.26 us  [sent(): return lax.ppermute(array, 'pulse', [(i, i ^ mask) for i in range(count)])]
  transfers between devices with their start and end apart: 5 -> 6, of which waited for: 1 -> 1; matrix products, arithmetic and copies ran while one was open for 0% -> 0% of each run, Pallas kernels for 23% -> 23%
where the time goes in v4:
time: 25 us; the launch traced here: 24.8 us
  starting transfers between devices  11.6 us (46%)
  Pallas kernels  10.5 us (42%)
  local copies, waits for them, and re-layouts  2.26 us (9%)
  waiting for transfers between devices  0.26 us (1%)
    ppermute x5, starting transfers between devices, sent(): return lax.ppermute(array, 'pulse', [(i, i ^ mask) for i in range(count)])  8.57 us
    pallas_call x1, Pallas kernels, body(): pl.pallas_call(second_kernel(bins), out_shape=jax.ShapeDtypeStruct((2, TW...  4.85 us
    pallas_call x1, Pallas kernels, body(): pl.pallas_call(first_kernel(bins), out_shape=jax.ShapeDtypeStruct((TWO, R...  3.53 us
    ppermute x1, starting transfers between devices, neighbours(): first = lax.ppermute(jnp.where(even, tail, head), axis, near)  3.03 us
    pallas_call x1, Pallas kernels, body(): pl.pallas_call(prep_kernel(bins), out_shape=(jax.ShapeDtypeStruct((span,...  2.09 us
    broadcast_in_dim x1, local copies, waits for them, and re-layouts, body(): return image.transpose(1, 0, 2)[None, None]  1.15 us
    unnamed x1, local copies, waits for them, and re-layouts  1.06 us
  transfers between devices with their start and end apart: 6, of which 1 were waited for; matrix products, arithmetic and copies ran while one was open for 0% of the time, Pallas kernels for 23%

profile of v4, /device:TPU:0, one launch (start us, length us, event | category | flops | bytes accessed | tf_op | source)
XLA Modules:
  0.0 24.8 jit_solution(14008072988536016282)
XLA Ops:
  0.0 1.1 %copy.20 = bf16[1,32,2,3072]{3,1,2,0:T(8,128)(2,1)S(1)} copy(bf16[1,32,2,3072]{3,2,1,0:T(2,128)(2,1)} %param.10) | data formatting | bytes 786432 | tf_op args[0]
  1.1 3.0 %collective-permute-start = (bf16[4,2,8,640]{3,2,0,1:T(8,128)(2,1)S(1)}, bf16[4,2,8,640]{3,2,0,1:T(8,128)(2,1)S(1)}, u32[]{:S(2)}, u32[]{:S(2)}) collective-permute-start(bf16[4,2,8,640]{3,2,0,1:T(8,128)(2,1)S(1)} %slice_select_fusion), channel_id=1, source_target_pairs={{0,2},{2,0},{1,3},{3,1},{4,6},{6,4},{5,7},{7,5},{8,10},{10,8},{9,1... | collective-permute-start | bytes 245768 | tf_op jit(solution)/shard_map/ppermute | solution.py:353
  4.1 1.6 %collective-permute-start.4 = (bf16[2,8,3072]{2,1,0:T(8,128)(2,1)S(1)}, bf16[2,8,3072]{2,1,0:T(8,128)(2,1)S(1)}, u32[]{:S(2)}, u32[]{:S(2)}) collective-permute-start(bf16[2,8,3072]{2,1,0:T(8,128)(2,1)S(1)} %get-tuple-element.13), channel_id=1, source_target_pairs={{0,4},{4,0},{8,12},{12,8},{1,5},{5,1},{9,13},{13,9},{2,6},{6,2},{1... | collective-permute-start | bytes 294920 | tf_op jit(solution)/shard_map/ppermute | solution.py:380
  5.8 2.5 %collective-permute-start.2 = (bf16[2,8,3072]{2,1,0:T(8,128)(2,1)S(1)}, bf16[2,8,3072]{2,1,0:T(8,128)(2,1)S(1)}, u32[]{:S(2)}, u32[]{:S(2)}) collective-permute-start(bf16[2,8,3072]{2,1,0:T(8,128)(2,1)S(1)} %get-tuple-element.14), channel_id=1, source_target_pairs={{0,12},{4,8},{8,4},{12,0},{1,13},{5,9},{9,5},{13,1},{2,14},{6,10},... | collective-permute-start | bytes 294920 | tf_op jit(solution)/shard_map/ppermute | solution.py:380
  8.3 0.0 collective-permute-done
  8.4 1.5 %collective-permute-start.1 = (bf16[2,8,3840]{2,1,0:T(8,128)(2,1)S(1)}, bf16[2,8,3840]{2,1,0:T(8,128)(2,1)S(1)}, u32[]{:S(2)}, u32[]{:S(2)}) collective-permute-start(bf16[2,8,3840]{2,1,0:T(8,128)(2,1)S(1)} %get-tuple-element.12), channel_id=1, source_target_pairs={{0,8},{4,12},{8,0},{12,4},{1,9},{5,13},{9,1},{13,5},{2,10},{6,14},... | collective-permute-start | bytes 368648 | tf_op jit(solution)/shard_map/ppermute | solution.py:380
  9.8 1.6 %collective-permute-start.5 = (bf16[2,8,768]{2,1,0:T(8,128)(2,1)S(1)}, bf16[2,8,768]{2,1,0:T(8,128)(2,1)S(1)}, u32[]{:S(2)}, u32[]{:S(2)}) collective-permute-start(bf16[2,8,768]{2,1,0:T(8,128)(2,1)S(1)} %get-tuple-element.17), channel_id=1, source_target_pairs={{0,4},{4,0},{8,12},{12,8},{1,5},{5,1},{9,13},{13,9},{2,6},{6,2},{1... | collective-permute-start | bytes 73736 | tf_op jit(solution)/shard_map/ppermute | solution.py:380
  11.4 1.4 %collective-permute-start.3 = (bf16[2,8,768]{2,1,0:T(8,128)(2,1)S(1)}, bf16[2,8,768]{2,1,0:T(8,128)(2,1)S(1)}, u32[]{:S(2)}, u32[]{:S(2)}) collective-permute-start(bf16[2,8,768]{2,1,0:T(8,128)(2,1)S(1)} %get-tuple-element.18), channel_id=1, source_target_pairs={{0,12},{4,8},{8,4},{12,0},{1,13},{5,9},{9,5},{13,1},{2,14},{6,10},... | collective-permute-start | bytes 73736 | tf_op jit(solution)/shard_map/ppermute | solution.py:380
  12.8 2.1 %prepare.1 = (bf16[640,256]{1,0:T(8,128)(2,1)S(1)}, f32[96,8,128]{2,1,0:T(8,128)S(1)}, f32[96,2,56,128]{3,2,1,0:T(8,128)S(1)}) custom-call(bf16[2,512]{1,0:T(2,128)(2,1)} %refs_0_.1, s32[2,128]{1,0:T(2,128)} %far_shift_one.3, f32[2,128]{1,0:T(2,128)} %refs_2_.1, f32[2,128]{1,0:T(2,128)} %refs_3_.1, s32[2,256]{1,0:T(2,128)} %far_shift_two.3, ...), custom_call_target="tpu_custom_call" | custom-call | tf_op jit(solution)/shard_map/prepare/pallas_call | solution.py:404
  14.9 0.0 collective-permute-done.4.a1
  14.9 0.0 collective-permute-done.5.r1
  15.0 3.5 %first_pair.1.half_ref = f32[32,56,128]{2,1,0:T(8,128)S(1)} custom-call(s32[2,128]{1,0:T(2,128)} %far_beam_one.3, s32[2,128]{1,0:T(2,128)} %far_shift_one.3, s32[2,256]{1,0:T(2,128)} %far_beam_two.3, s32[2,256]{1,0:T(2,128)} %far_shift_two.3, bf16[2,8,3840]{2,1,0:T(8,128)(2,1)S(1)} %get-tuple-element.11.a0, ...), custom_call_target="tpu_custom_call" | custom-call | tf_op jit(solution)/shard_map/first_pair/pallas_call | solution.py:427
  18.5 0.0 collective-permute-done.2.a3
  18.5 0.0 collective-permute-done.3.r3
  18.5 0.2 %collective-permute-done.1.a2 = bf16[2,8,3840]{2,1,0:T(8,128)(2,1)S(1)} collective-permute-done((bf16[2,8,3840]{2,1,0:T(8,128)(2,1)S(1)}, bf16[2,8,3840]{2,1,0:T(8,128)(2,1)S(1)}, u32[]{:S(2)}, u32[]{:S(2)}) %collective-permute-start.1) | collective-permute-done | bytes 122912 | tf_op jit(solution)/shard_map/ppermute | solution.py:380
  18.8 4.8 %second_pair.1 = bf16[2,32,3072]{2,1,0:T(8,128)(2,1)S(1)} custom-call(s32[2,128]{1,0:T(2,128)} %far_beam_one.3, s32[2,128]{1,0:T(2,128)} %far_shift_one.3, s32[2,256]{1,0:T(2,128)} %far_beam_two.3, s32[2,256]{1,0:T(2,128)} %far_shift_two.3, bf16[2,8,3840]{2,1,0:T(8,128)(2,1)S(1)} %collective-permute-done.1.a2, ...), custom_call_target="tpu_custom_call" | custom-call | tf_op jit(solution)/shard_map/second_pair/pallas_call | solution.py:436
  23.6 1.2 %copy.15 = bf16[1,1,32,2,3072]{4,3,2,1,0:T(2,128)(2,1)} copy(bf16[1,1,32,2,3072]{4,2,3,1,0:T(8,128)(2,1)S(1)} %bitcast.29) | data formatting | bytes 786432 | tf_op jit(solution)/shard_map/broadcast_in_dim | solution.py:445
  (7 shorter events, 0.1 us)
Async XLA Ops:
  1.1 7.2 %collective-permute-start = (bf16[4,2,8,640]{3,2,0,1:T(8,128)(2,1)S(1)}, bf16[4,2,8,640]{3,2,0,1:T(8,128)(2,1)S(1)}, u32[]{:S(2)}, u32[]{:S(2)}) collective-permute-start(bf16[4,2,8,640]{3,2,0,1:T(8,128)(2,1)S(1)} %slice_select_fusion), channel_id=1, source_target_pairs={{0,2},{2,0},{1,3},{3,1},{4,6},{6,4},{5,7},{7,5},{8,10},{10,8},{9,1... | collective-permute-start | bytes 245768 | tf_op jit(solution)/shard_map/ppermute | solution.py:353
  4.1 10.8 %collective-permute-start.4 = (bf16[2,8,3072]{2,1,0:T(8,128)(2,1)S(1)}, bf16[2,8,3072]{2,1,0:T(8,128)(2,1)S(1)}, u32[]{:S(2)}, u32[]{:S(2)}) collective-permute-start(bf16[2,8,3072]{2,1,0:T(8,128)(2,1)S(1)} %get-tuple-element.13), channel_id=1, source_target_pairs={{0,4},{4,0},{8,12},{12,8},{1,5},{5,1},{9,13},{13,9},{2,6},{6,2},{1... | collective-permute-start | bytes 294920 | tf_op jit(solution)/shard_map/ppermute | solution.py:380
  5.8 12.7 %collective-permute-start.2 = (bf16[2,8,3072]{2,1,0:T(8,128)(2,1)S(1)}, bf16[2,8,3072]{2,1,0:T(8,128)(2,1)S(1)}, u32[]{:S(2)}, u32[]{:S(2)}) collective-permute-start(bf16[2,8,3072]{2,1,0:T(8,128)(2,1)S(1)} %get-tuple-element.14), channel_id=1, source_target_pairs={{0,12},{4,8},{8,4},{12,0},{1,13},{5,9},{9,5},{13,1},{2,14},{6,10},... | collective-permute-start | bytes 294920 | tf_op jit(solution)/shard_map/ppermute | solution.py:380
  8.4 10.4 %collective-permute-start.1 = (bf16[2,8,3840]{2,1,0:T(8,128)(2,1)S(1)}, bf16[2,8,3840]{2,1,0:T(8,128)(2,1)S(1)}, u32[]{:S(2)}, u32[]{:S(2)}) collective-permute-start(bf16[2,8,3840]{2,1,0:T(8,128)(2,1)S(1)} %get-tuple-element.12), channel_id=1, source_target_pairs={{0,8},{4,12},{8,0},{12,4},{1,9},{5,13},{9,1},{13,5},{2,10},{6,14},... | collective-permute-start | bytes 368648 | tf_op jit(solution)/shard_map/ppermute | solution.py:380
  9.8 5.1 %collective-permute-start.5 = (bf16[2,8,768]{2,1,0:T(8,128)(2,1)S(1)}, bf16[2,8,768]{2,1,0:T(8,128)(2,1)S(1)}, u32[]{:S(2)}, u32[]{:S(2)}) collective-permute-start(bf16[2,8,768]{2,1,0:T(8,128)(2,1)S(1)} %get-tuple-element.17), channel_id=1, source_target_pairs={{0,4},{4,0},{8,12},{12,8},{1,5},{5,1},{9,13},{13,9},{2,6},{6,2},{1... | collective-permute-start | bytes 73736 | tf_op jit(solution)/shard_map/ppermute | solution.py:380
  11.4 7.1 %collective-permute-start.3 = (bf16[2,8,768]{2,1,0:T(8,128)(2,1)S(1)}, bf16[2,8,768]{2,1,0:T(8,128)(2,1)S(1)}, u32[]{:S(2)}, u32[]{:S(2)}) collective-permute-start(bf16[2,8,768]{2,1,0:T(8,128)(2,1)S(1)} %get-tuple-element.18), channel_id=1, source_target_pairs={{0,12},{4,8},{8,4},{12,0},{1,13},{5,9},{9,5},{13,1},{2,14},{6,10},... | collective-permute-start | bytes 73736 | tf_op jit(solution)/shard_map/ppermute | solution.py:380

commit v5 on v4

--- a/solution.py
+++ b/solution.py
@@ -161,11 +161,18 @@
             sin_all = jnp.broadcast_to(sin_col[place : place + 1], shape) * sign
             cos_step, sin_step = spread_out(cos_fine), spread_out(sin_fine) * sign
             cos_next, sin_next = spread_out(cos_coarse), spread_out(sin_coarse) * sign
+            twice = cos_next + cos_next
+            before = None
             for chunk in range(CHUNKS):
-                cos_all, sin_all = (
-                    cos_all * cos_step - sin_all * sin_step,
-                    sin_all * cos_step + cos_all * sin_step,
-                )
+                if chunk < 2:
+                    now = (
+                        cos_all * cos_step - sin_all * sin_step,
+                        sin_all * cos_step + cos_all * sin_step,
+                    )
+                else:
+                    now = (twice * cos_all - before[0], twice * sin_all - before[1])
+                before = (cos_all, sin_all)
+                cos_all, sin_all = now
                 turn_ref[place, 0, pl.ds(8 * chunk, 8), :] = cos_all
                 turn_ref[place, 1, pl.ds(8 * chunk, 8), :] = sin_all
                 cos_step, sin_step = cos_next, sin_next

time: 25 us -> 25 us (level)
  transfers between devices with their start and end apart: 6 -> 6, of which waited for: 1 -> 1; matrix products, arithmetic and copies ran while one was open for 0% -> 0% of each run, Pallas kernels for 23% -> 22%
where the time goes in v5:
time: 25 us; the launch traced here: 24.8 us
  starting transfers between devices  11.6 us (46%)
  Pallas kernels  10.4 us (42%)
  local copies, waits for them, and re-layouts  2.26 us (9%)
  waiting for transfers between devices  0.33 us (1%)
    ppermute x5, starting transfers between devices, sent(): return lax.ppermute(array, 'pulse', [(i, i ^ mask) for i in range(count)])  8.57 us
    pallas_call x1, Pallas kernels, body(): pl.pallas_call(second_kernel(bins), out_shape=jax.ShapeDtypeStruct((2, TW...  4.85 us
    pallas_call x1, Pallas kernels, body(): pl.pallas_call(first_kernel(bins), out_shape=jax.ShapeDtypeStruct((TWO, R...  3.53 us
    ppermute x1, starting transfers between devices, neighbours(): first = lax.ppermute(jnp.where(even, tail, head), axis, near)  3.03 us
    pallas_call x1, Pallas kernels, body(): pl.pallas_call(prep_kernel(bins), out_shape=(jax.ShapeDtypeStruct((span,...  2.03 us
    broadcast_in_dim x1, local copies, waits for them, and re-layouts, body(): return image.transpose(1, 0, 2)[None, None]  1.15 us
    unnamed x1, local copies, waits for them, and re-layouts  1.06 us
  transfers between devices with their start and end apart: 6, of which 1 were waited for; matrix products, arithmetic and copies ran while one was open for 0% of the time, Pallas kernels for 22%

profile of v5, /device:TPU:0, one launch (start us, length us, event | category | flops | bytes accessed | tf_op | source)
XLA Modules:
  0.0 24.8 jit_solution(15828583228040323060)
XLA Ops:
  0.0 1.1 %copy.20 = bf16[1,32,2,3072]{3,1,2,0:T(8,128)(2,1)S(1)} copy(bf16[1,32,2,3072]{3,2,1,0:T(2,128)(2,1)} %param.10) | data formatting | bytes 786432 | tf_op args[0]
  1.1 3.0 %collective-permute-start = (bf16[4,2,8,640]{3,2,0,1:T(8,128)(2,1)S(1)}, bf16[4,2,8,640]{3,2,0,1:T(8,128)(2,1)S(1)}, u32[]{:S(2)}, u32[]{:S(2)}) collective-permute-start(bf16[4,2,8,640]{3,2,0,1:T(8,128)(2,1)S(1)} %slice_select_fusion), channel_id=1, source_target_pairs={{0,2},{2,0},{1,3},{3,1},{4,6},{6,4},{5,7},{7,5},{8,10},{10,8},{9,1... | collective-permute-start | bytes 245768 | tf_op jit(solution)/shard_map/ppermute | solution.py:360
  4.1 1.6 %collective-permute-start.4 = (bf16[2,8,3072]{2,1,0:T(8,128)(2,1)S(1)}, bf16[2,8,3072]{2,1,0:T(8,128)(2,1)S(1)}, u32[]{:S(2)}, u32[]{:S(2)}) collective-permute-start(bf16[2,8,3072]{2,1,0:T(8,128)(2,1)S(1)} %get-tuple-element.13), channel_id=1, source_target_pairs={{0,4},{4,0},{8,12},{12,8},{1,5},{5,1},{9,13},{13,9},{2,6},{6,2},{1... | collective-permute-start | bytes 294920 | tf_op jit(solution)/shard_map/ppermute | solution.py:387
  5.8 2.5 %collective-permute-start.2 = (bf16[2,8,3072]{2,1,0:T(8,128)(2,1)S(1)}, bf16[2,8,3072]{2,1,0:T(8,128)(2,1)S(1)}, u32[]{:S(2)}, u32[]{:S(2)}) collective-permute-start(bf16[2,8,3072]{2,1,0:T(8,128)(2,1)S(1)} %get-tuple-element.14), channel_id=1, source_target_pairs={{0,12},{4,8},{8,4},{12,0},{1,13},{5,9},{9,5},{13,1},{2,14},{6,10},... | collective-permute-start | bytes 294920 | tf_op jit(solution)/shard_map/ppermute | solution.py:387
  8.3 0.0 collective-permute-done
  8.4 1.5 %collective-permute-start.1 = (bf16[2,8,3840]{2,1,0:T(8,128)(2,1)S(1)}, bf16[2,8,3840]{2,1,0:T(8,128)(2,1)S(1)}, u32[]{:S(2)}, u32[]{:S(2)}) collective-permute-start(bf16[2,8,3840]{2,1,0:T(8,128)(2,1)S(1)} %get-tuple-element.12), channel_id=1, source_target_pairs={{0,8},{4,12},{8,0},{12,4},{1,9},{5,13},{9,1},{13,5},{2,10},{6,14},... | collective-permute-start | bytes 368648 | tf_op jit(solution)/shard_map/ppermute | solution.py:387
  9.8 1.6 %collective-permute-start.5 = (bf16[2,8,768]{2,1,0:T(8,128)(2,1)S(1)}, bf16[2,8,768]{2,1,0:T(8,128)(2,1)S(1)}, u32[]{:S(2)}, u32[]{:S(2)}) collective-permute-start(bf16[2,8,768]{2,1,0:T(8,128)(2,1)S(1)} %get-tuple-element.17), channel_id=1, source_target_pairs={{0,4},{4,0},{8,12},{12,8},{1,5},{5,1},{9,13},{13,9},{2,6},{6,2},{1... | collective-permute-start | bytes 73736 | tf_op jit(solution)/shard_map/ppermute | solution.py:387
  11.4 1.4 %collective-permute-start.3 = (bf16[2,8,768]{2,1,0:T(8,128)(2,1)S(1)}, bf16[2,8,768]{2,1,0:T(8,128)(2,1)S(1)}, u32[]{:S(2)}, u32[]{:S(2)}) collective-permute-start(bf16[2,8,768]{2,1,0:T(8,128)(2,1)S(1)} %get-tuple-element.18), channel_id=1, source_target_pairs={{0,12},{4,8},{8,4},{12,0},{1,13},{5,9},{9,5},{13,1},{2,14},{6,10},... | collective-permute-start | bytes 73736 | tf_op jit(solution)/shard_map/ppermute | solution.py:387
  12.8 2.0 %prepare.1 = (bf16[640,256]{1,0:T(8,128)(2,1)S(1)}, f32[96,8,128]{2,1,0:T(8,128)S(1)}, f32[96,2,56,128]{3,2,1,0:T(8,128)S(1)}) custom-call(bf16[2,512]{1,0:T(2,128)(2,1)} %refs_0_.1, s32[2,128]{1,0:T(2,128)} %far_shift_one.3, f32[2,128]{1,0:T(2,128)} %refs_2_.1, f32[2,128]{1,0:T(2,128)} %refs_3_.1, s32[2,256]{1,0:T(2,128)} %far_shift_two.3, ...), custom_call_target="tpu_custom_call" | custom-call | tf_op jit(solution)/shard_map/prepare/pallas_call | solution.py:411
  14.9 0.0 collective-permute-done.4.a1
  14.9 0.0 collective-permute-done.5.r1
  14.9 3.5 %first_pair.1.half_ref = f32[32,56,128]{2,1,0:T(8,128)S(1)} custom-call(s32[2,128]{1,0:T(2,128)} %far_beam_one.3, s32[2,128]{1,0:T(2,128)} %far_shift_one.3, s32[2,256]{1,0:T(2,128)} %far_beam_two.3, s32[2,256]{1,0:T(2,128)} %far_shift_two.3, bf16[2,8,3840]{2,1,0:T(8,128)(2,1)S(1)} %get-tuple-element.11.a0, ...), custom_call_target="tpu_custom_call" | custom-call | tf_op jit(solution)/shard_map/first_pair/pallas_call | solution.py:434
  18.4 0.0 collective-permute-done.2.a3
  18.4 0.0 collective-permute-done.3.r3
  18.4 0.3 %collective-permute-done.1.a2 = bf16[2,8,3840]{2,1,0:T(8,128)(2,1)S(1)} collective-permute-done((bf16[2,8,3840]{2,1,0:T(8,128)(2,1)S(1)}, bf16[2,8,3840]{2,1,0:T(8,128)(2,1)S(1)}, u32[]{:S(2)}, u32[]{:S(2)}) %collective-permute-start.1) | collective-permute-done | bytes 122912 | tf_op jit(solution)/shard_map/ppermute | solution.py:387
  18.8 4.8 %second_pair.1 = bf16[2,32,3072]{2,1,0:T(8,128)(2,1)S(1)} custom-call(s32[2,128]{1,0:T(2,128)} %far_beam_one.3, s32[2,128]{1,0:T(2,128)} %far_shift_one.3, s32[2,256]{1,0:T(2,128)} %far_beam_two.3, s32[2,256]{1,0:T(2,128)} %far_shift_two.3, bf16[2,8,3840]{2,1,0:T(8,128)(2,1)S(1)} %collective-permute-done.1.a2, ...), custom_call_target="tpu_custom_call" | custom-call | tf_op jit(solution)/shard_map/second_pair/pallas_call | solution.py:443
  23.6 1.2 %copy.15 = bf16[1,1,32,2,3072]{4,3,2,1,0:T(2,128)(2,1)} copy(bf16[1,1,32,2,3072]{4,2,3,1,0:T(8,128)(2,1)S(1)} %bitcast.29) | data formatting | bytes 786432 | tf_op jit(solution)/shard_map/broadcast_in_dim | solution.py:452
  (7 shorter events, 0.1 us)
Async XLA Ops:
  1.1 7.2 %collective-permute-start = (bf16[4,2,8,640]{3,2,0,1:T(8,128)(2,1)S(1)}, bf16[4,2,8,640]{3,2,0,1:T(8,128)(2,1)S(1)}, u32[]{:S(2)}, u32[]{:S(2)}) collective-permute-start(bf16[4,2,8,640]{3,2,0,1:T(8,128)(2,1)S(1)} %slice_select_fusion), channel_id=1, source_target_pairs={{0,2},{2,0},{1,3},{3,1},{4,6},{6,4},{5,7},{7,5},{8,10},{10,8},{9,1... | collective-permute-start | bytes 245768 | tf_op jit(solution)/shard_map/ppermute | solution.py:360
  4.1 10.7 %collective-permute-start.4 = (bf16[2,8,3072]{2,1,0:T(8,128)(2,1)S(1)}, bf16[2,8,3072]{2,1,0:T(8,128)(2,1)S(1)}, u32[]{:S(2)}, u32[]{:S(2)}) collective-permute-start(bf16[2,8,3072]{2,1,0:T(8,128)(2,1)S(1)} %get-tuple-element.13), channel_id=1, source_target_pairs={{0,4},{4,0},{8,12},{12,8},{1,5},{5,1},{9,13},{13,9},{2,6},{6,2},{1... | collective-permute-start | bytes 294920 | tf_op jit(solution)/shard_map/ppermute | solution.py:387
  5.8 12.7 %collective-permute-start.2 = (bf16[2,8,3072]{2,1,0:T(8,128)(2,1)S(1)}, bf16[2,8,3072]{2,1,0:T(8,128)(2,1)S(1)}, u32[]{:S(2)}, u32[]{:S(2)}) collective-permute-start(bf16[2,8,3072]{2,1,0:T(8,128)(2,1)S(1)} %get-tuple-element.14), channel_id=1, source_target_pairs={{0,12},{4,8},{8,4},{12,0},{1,13},{5,9},{9,5},{13,1},{2,14},{6,10},... | collective-permute-start | bytes 294920 | tf_op jit(solution)/shard_map/ppermute | solution.py:387
  8.4 10.4 %collective-permute-start.1 = (bf16[2,8,3840]{2,1,0:T(8,128)(2,1)S(1)}, bf16[2,8,3840]{2,1,0:T(8,128)(2,1)S(1)}, u32[]{:S(2)}, u32[]{:S(2)}) collective-permute-start(bf16[2,8,3840]{2,1,0:T(8,128)(2,1)S(1)} %get-tuple-element.12), channel_id=1, source_target_pairs={{0,8},{4,12},{8,0},{12,4},{1,9},{5,13},{9,1},{13,5},{2,10},{6,14},... | collective-permute-start | bytes 368648 | tf_op jit(solution)/shard_map/ppermute | solution.py:387
  9.8 5.0 %collective-permute-start.5 = (bf16[2,8,768]{2,1,0:T(8,128)(2,1)S(1)}, bf16[2,8,768]{2,1,0:T(8,128)(2,1)S(1)}, u32[]{:S(2)}, u32[]{:S(2)}) collective-permute-start(bf16[2,8,768]{2,1,0:T(8,128)(2,1)S(1)} %get-tuple-element.17), channel_id=1, source_target_pairs={{0,4},{4,0},{8,12},{12,8},{1,5},{5,1},{9,13},{13,9},{2,6},{6,2},{1... | collective-permute-start | bytes 73736 | tf_op jit(solution)/shard_map/ppermute | solution.py:387
  11.4 7.0 %collective-permute-start.3 = (bf16[2,8,768]{2,1,0:T(8,128)(2,1)S(1)}, bf16[2,8,768]{2,1,0:T(8,128)(2,1)S(1)}, u32[]{:S(2)}, u32[]{:S(2)}) collective-permute-start(bf16[2,8,768]{2,1,0:T(8,128)(2,1)S(1)} %get-tuple-element.18), channel_id=1, source_target_pairs={{0,12},{4,8},{8,4},{12,0},{1,13},{5,9},{9,5},{13,1},{2,14},{6,10},... | collective-permute-start | bytes 73736 | tf_op jit(solution)/shard_map/ppermute | solution.py:387

commit v6 on v5

--- a/solution.py
+++ b/solution.py
@@ -17,7 +17,7 @@
 BLOCKS = WIDE // STEP
 ONE, TWO = 16, 32
 TALL = ROWS + 2 * RIM
-TOGETHER = 16
+TOGETHER = 32
 
 
 def position():
@@ -250,12 +250,14 @@
 
 
 def loop_over(count, one):
+    size = min(TOGETHER, count)
+
     def step(index, carry):
-        for extra in range(TOGETHER):
-            one(TOGETHER * index + extra)
+        for extra in range(size):
+            one(size * index + extra)
         return carry
 
-    lax.fori_loop(0, count // TOGETHER, step, 0)
+    lax.fori_loop(0, count // size, step, 0)
 
 
 def merge_one(images, tables, result, inside):

time: 25 us -> 25.3 us (1.012)
  Pallas kernels: 10.4 us -> 10.9 us
    pallas_call x1, Pallas kernels: 4.85 us -> 5.15 us  [body(): pl.pallas_call(second_kernel(bins), out_shape=jax.ShapeDtypeStruct((2, TW...]
  transfers between devices with their start and end apart: 6 -> 6, of which waited for: 1 -> 1; matrix products, arithmetic and copies ran while one was open for 0% -> 0% of each run, Pallas kernels for 22% -> 23%
where the time goes in v6:
time: 25.3 us; the launch traced here: 25.1 us
  starting transfers between devices  11.6 us (46%)
  Pallas kernels  10.9 us (43%)
  local copies, waits for them, and re-layouts  2.26 us (9%)
    ppermute x5, starting transfers between devices, sent(): return lax.ppermute(array, 'pulse', [(i, i ^ mask) for i in range(count)])  8.57 us
    pallas_call x1, Pallas kernels, body(): pl.pallas_call(second_kernel(bins), out_shape=jax.ShapeDtypeStruct((2, TW...  5.15 us
    pallas_call x1, Pallas kernels, body(): pl.pallas_call(first_kernel(bins), out_shape=jax.ShapeDtypeStruct((TWO, R...  3.68 us
    ppermute x1, starting transfers between devices, neighbours(): first = lax.ppermute(jnp.where(even, tail, head), axis, near)  3.03 us
    pallas_call x1, Pallas kernels, body(): pl.pallas_call(prep_kernel(bins), out_shape=(jax.ShapeDtypeStruct((span,...  2.03 us
    broadcast_in_dim x1, local copies, waits for them, and re-layouts, body(): return image.transpose(1, 0, 2)[None, None]  1.15 us
    unnamed x1, local copies, waits for them, and re-layouts  1.06 us
  transfers between devices with their start and end apart: 6, of which 1 were waited for; matrix products, arithmetic and copies ran while one was open for 0% of the time, Pallas kernels for 23%

profile of v6, /device:TPU:0, one launch (start us, length us, event | category | flops | bytes accessed | tf_op | source)
XLA Modules:
  0.0 25.1 jit_solution(2635442981994388652)
XLA Ops:
  0.0 1.1 %copy.20 = bf16[1,32,2,3072]{3,1,2,0:T(8,128)(2,1)S(1)} copy(bf16[1,32,2,3072]{3,2,1,0:T(2,128)(2,1)} %param.10) | data formatting | bytes 786432 | tf_op args[0]
  1.1 3.0 %collective-permute-start = (bf16[4,2,8,640]{3,2,0,1:T(8,128)(2,1)S(1)}, bf16[4,2,8,640]{3,2,0,1:T(8,128)(2,1)S(1)}, u32[]{:S(2)}, u32[]{:S(2)}) collective-permute-start(bf16[4,2,8,640]{3,2,0,1:T(8,128)(2,1)S(1)} %slice_select_fusion), channel_id=1, source_target_pairs={{0,2},{2,0},{1,3},{3,1},{4,6},{6,4},{5,7},{7,5},{8,10},{10,8},{9,1... | collective-permute-start | bytes 245768 | tf_op jit(solution)/shard_map/ppermute | solution.py:362
  4.1 1.6 %collective-permute-start.4 = (bf16[2,8,3072]{2,1,0:T(8,128)(2,1)S(1)}, bf16[2,8,3072]{2,1,0:T(8,128)(2,1)S(1)}, u32[]{:S(2)}, u32[]{:S(2)}) collective-permute-start(bf16[2,8,3072]{2,1,0:T(8,128)(2,1)S(1)} %get-tuple-element.13), channel_id=1, source_target_pairs={{0,4},{4,0},{8,12},{12,8},{1,5},{5,1},{9,13},{13,9},{2,6},{6,2},{1... | collective-permute-start | bytes 294920 | tf_op jit(solution)/shard_map/ppermute | solution.py:389
  5.8 2.5 %collective-permute-start.2 = (bf16[2,8,3072]{2,1,0:T(8,128)(2,1)S(1)}, bf16[2,8,3072]{2,1,0:T(8,128)(2,1)S(1)}, u32[]{:S(2)}, u32[]{:S(2)}) collective-permute-start(bf16[2,8,3072]{2,1,0:T(8,128)(2,1)S(1)} %get-tuple-element.14), channel_id=1, source_target_pairs={{0,12},{4,8},{8,4},{12,0},{1,13},{5,9},{9,5},{13,1},{2,14},{6,10},... | collective-permute-start | bytes 294920 | tf_op jit(solution)/shard_map/ppermute | solution.py:389
  8.3 0.0 collective-permute-done
  8.4 1.5 %collective-permute-start.1 = (bf16[2,8,3840]{2,1,0:T(8,128)(2,1)S(1)}, bf16[2,8,3840]{2,1,0:T(8,128)(2,1)S(1)}, u32[]{:S(2)}, u32[]{:S(2)}) collective-permute-start(bf16[2,8,3840]{2,1,0:T(8,128)(2,1)S(1)} %get-tuple-element.12), channel_id=1, source_target_pairs={{0,8},{4,12},{8,0},{12,4},{1,9},{5,13},{9,1},{13,5},{2,10},{6,14},... | collective-permute-start | bytes 368648 | tf_op jit(solution)/shard_map/ppermute | solution.py:389
  9.8 1.6 %collective-permute-start.5 = (bf16[2,8,768]{2,1,0:T(8,128)(2,1)S(1)}, bf16[2,8,768]{2,1,0:T(8,128)(2,1)S(1)}, u32[]{:S(2)}, u32[]{:S(2)}) collective-permute-start(bf16[2,8,768]{2,1,0:T(8,128)(2,1)S(1)} %get-tuple-element.17), channel_id=1, source_target_pairs={{0,4},{4,0},{8,12},{12,8},{1,5},{5,1},{9,13},{13,9},{2,6},{6,2},{1... | collective-permute-start | bytes 73736 | tf_op jit(solution)/shard_map/ppermute | solution.py:389
  11.4 1.4 %collective-permute-start.3 = (bf16[2,8,768]{2,1,0:T(8,128)(2,1)S(1)}, bf16[2,8,768]{2,1,0:T(8,128)(2,1)S(1)}, u32[]{:S(2)}, u32[]{:S(2)}) collective-permute-start(bf16[2,8,768]{2,1,0:T(8,128)(2,1)S(1)} %get-tuple-element.18), channel_id=1, source_target_pairs={{0,12},{4,8},{8,4},{12,0},{1,13},{5,9},{9,5},{13,1},{2,14},{6,10},... | collective-permute-start | bytes 73736 | tf_op jit(solution)/shard_map/ppermute | solution.py:389
  12.8 2.0 %prepare.1 = (bf16[640,256]{1,0:T(8,128)(2,1)S(1)}, f32[96,8,128]{2,1,0:T(8,128)S(1)}, f32[96,2,56,128]{3,2,1,0:T(8,128)S(1)}) custom-call(bf16[2,512]{1,0:T(2,128)(2,1)} %refs_0_.1, s32[2,128]{1,0:T(2,128)} %far_shift_one.3, f32[2,128]{1,0:T(2,128)} %refs_2_.1, f32[2,128]{1,0:T(2,128)} %refs_3_.1, s32[2,256]{1,0:T(2,128)} %far_shift_two.3, ...), custom_call_target="tpu_custom_call" | custom-call | tf_op jit(solution)/shard_map/prepare/pallas_call | solution.py:413
  14.9 0.0 collective-permute-done.4.a1
  14.9 0.0 collective-permute-done.5.r1
  14.9 3.7 %first_pair.1.half_ref = f32[32,56,128]{2,1,0:T(8,128)S(1)} custom-call(s32[2,128]{1,0:T(2,128)} %far_beam_one.3, s32[2,128]{1,0:T(2,128)} %far_shift_one.3, s32[2,256]{1,0:T(2,128)} %far_beam_two.3, s32[2,256]{1,0:T(2,128)} %far_shift_two.3, bf16[2,8,3840]{2,1,0:T(8,128)(2,1)S(1)} %get-tuple-element.11.a0, ...), custom_call_target="tpu_custom_call" | custom-call | tf_op jit(solution)/shard_map/first_pair/pallas_call | solution.py:436
  18.6 0.0 collective-permute-done.2.a3
  18.6 0.0 collective-permute-done.3.r3
  18.6 0.2 collective-permute-done.1.a2
  18.8 5.1 %second_pair.1 = bf16[2,32,3072]{2,1,0:T(8,128)(2,1)S(1)} custom-call(s32[2,128]{1,0:T(2,128)} %far_beam_one.3, s32[2,128]{1,0:T(2,128)} %far_shift_one.3, s32[2,256]{1,0:T(2,128)} %far_beam_two.3, s32[2,256]{1,0:T(2,128)} %far_shift_two.3, bf16[2,8,3840]{2,1,0:T(8,128)(2,1)S(1)} %collective-permute-done.1.a2, ...), custom_call_target="tpu_custom_call" | custom-call | tf_op jit(solution)/shard_map/second_pair/pallas_call | solution.py:445
  23.9 1.2 %copy.15 = bf16[1,1,32,2,3072]{4,3,2,1,0:T(2,128)(2,1)} copy(bf16[1,1,32,2,3072]{4,2,3,1,0:T(8,128)(2,1)S(1)} %bitcast.29) | data formatting | bytes 786432 | tf_op jit(solution)/shard_map/broadcast_in_dim | solution.py:454
  (7 shorter events, 0.1 us)
Async XLA Ops:
  1.1 7.2 %collective-permute-start = (bf16[4,2,8,640]{3,2,0,1:T(8,128)(2,1)S(1)}, bf16[4,2,8,640]{3,2,0,1:T(8,128)(2,1)S(1)}, u32[]{:S(2)}, u32[]{:S(2)}) collective-permute-start(bf16[4,2,8,640]{3,2,0,1:T(8,128)(2,1)S(1)} %slice_select_fusion), channel_id=1, source_target_pairs={{0,2},{2,0},{1,3},{3,1},{4,6},{6,4},{5,7},{7,5},{8,10},{10,8},{9,1... | collective-permute-start | bytes 245768 | tf_op jit(solution)/shard_map/ppermute | solution.py:362
  4.1 10.7 %collective-permute-start.4 = (bf16[2,8,3072]{2,1,0:T(8,128)(2,1)S(1)}, bf16[2,8,3072]{2,1,0:T(8,128)(2,1)S(1)}, u32[]{:S(2)}, u32[]{:S(2)}) collective-permute-start(bf16[2,8,3072]{2,1,0:T(8,128)(2,1)S(1)} %get-tuple-element.13), channel_id=1, source_target_pairs={{0,4},{4,0},{8,12},{12,8},{1,5},{5,1},{9,13},{13,9},{2,6},{6,2},{1... | collective-permute-start | bytes 294920 | tf_op jit(solution)/shard_map/ppermute | solution.py:389
  5.8 12.8 %collective-permute-start.2 = (bf16[2,8,3072]{2,1,0:T(8,128)(2,1)S(1)}, bf16[2,8,3072]{2,1,0:T(8,128)(2,1)S(1)}, u32[]{:S(2)}, u32[]{:S(2)}) collective-permute-start(bf16[2,8,3072]{2,1,0:T(8,128)(2,1)S(1)} %get-tuple-element.14), channel_id=1, source_target_pairs={{0,12},{4,8},{8,4},{12,0},{1,13},{5,9},{9,5},{13,1},{2,14},{6,10},... | collective-permute-start | bytes 294920 | tf_op jit(solution)/shard_map/ppermute | solution.py:389
  8.4 10.4 %collective-permute-start.1 = (bf16[2,8,3840]{2,1,0:T(8,128)(2,1)S(1)}, bf16[2,8,3840]{2,1,0:T(8,128)(2,1)S(1)}, u32[]{:S(2)}, u32[]{:S(2)}) collective-permute-start(bf16[2,8,3840]{2,1,0:T(8,128)(2,1)S(1)} %get-tuple-element.12), channel_id=1, source_target_pairs={{0,8},{4,12},{8,0},{12,4},{1,9},{5,13},{9,1},{13,5},{2,10},{6,14},... | collective-permute-start | bytes 368648 | tf_op jit(solution)/shard_map/ppermute | solution.py:389
  9.8 5.0 %collective-permute-start.5 = (bf16[2,8,768]{2,1,0:T(8,128)(2,1)S(1)}, bf16[2,8,768]{2,1,0:T(8,128)(2,1)S(1)}, u32[]{:S(2)}, u32[]{:S(2)}) collective-permute-start(bf16[2,8,768]{2,1,0:T(8,128)(2,1)S(1)} %get-tuple-element.17), channel_id=1, source_target_pairs={{0,4},{4,0},{8,12},{12,8},{1,5},{5,1},{9,13},{13,9},{2,6},{6,2},{1... | collective-permute-start | bytes 73736 | tf_op jit(solution)/shard_map/ppermute | solution.py:389
  11.4 7.2 %collective-permute-start.3 = (bf16[2,8,768]{2,1,0:T(8,128)(2,1)S(1)}, bf16[2,8,768]{2,1,0:T(8,128)(2,1)S(1)}, u32[]{:S(2)}, u32[]{:S(2)}) collective-permute-start(bf16[2,8,768]{2,1,0:T(8,128)(2,1)S(1)} %get-tuple-element.18), channel_id=1, source_target_pairs={{0,12},{4,8},{8,4},{12,0},{1,13},{5,9},{9,5},{13,1},{2,14},{6,10},... | collective-permute-start | bytes 73736 | tf_op jit(solution)/shard_map/ppermute | solution.py:389
